TPU v7x, 128 devices: a whole 4x4x4 slice. The times are simulated.
128 devices in a mesh: split: 16 (over x, y_hi, core), shard: 8 (over y_lo, z).
Axes of the slice: x: 4, y: 4 (y_hi: 2, y_lo: 2; y = y_hi * 2 + y_lo), z: 4, core: 2. Of those that a mesh axis runs over, the one named last changes fastest.
Arguments:
- strain: bfloat16 [3, 4096], P(None, ('split', 'shard')), may hold values from -6 to 6
- basis: bfloat16 [16, 400, 2048], P('split', 'shard'), may hold values from -0.125 to 0.125
- recon: bfloat16 [16, 2, 4096, 400], P('split', None, 'shard'), may hold values from -0.3125 to 0.3125
Outputs:
- snr2: float32 [16, 4096, 2048], P('split', 'shard')
- loudest: float32 [2048], replicated
All inputs are finite; a program needn't handle non-finite values.
Results may differ from a plain program's by a relative error of at most 0.0025.
Values may be sent and summed in bfloat16 or wider, within the bound.
No kernel may reach another device: no remote copies, remote signals or barrier semaphores. Data moves between devices by JAX's collectives and lax.ppermute only.
A program may use at most 128 MiB of HBM per device.

v0:
```python
import jax
import jax.numpy as jnp
from jax import lax
from jax.sharding import PartitionSpec as P


def toeplitz_block(segment, rows, cols):
    width = rows + cols - 1
    turned = jnp.concatenate([segment[rows - 1 :], segment[: rows - 1]])
    flat = jnp.broadcast_to(turned, (rows, width)).reshape(-1)[: rows * (width - 1)]
    return flat.reshape(rows, width - 1)[:, :cols]


def filter_series(signal, filters):
    taps = filters.shape[1]
    tout = signal.shape[0] - taps
    tblock = min(512, tout)
    kblock = min(512, taps)
    outputs = []
    for tpos in range(tout // tblock):
        pieces = []
        for kpos in range(taps // kblock):
            begin = tpos * tblock + taps - (kpos + 1) * kblock
            segment = signal[begin : begin + kblock + tblock - 1]
            pieces.append(toeplitz_block(segment, kblock, tblock))
        frame = jnp.concatenate(pieces, axis=0)
        outputs.append(jnp.dot(filters, frame, preferred_element_type=jnp.float32))
    return jnp.concatenate(outputs, axis=1)


def all_detectors(whole, filters):
    return jnp.stack(
        [filter_series(whole[det], filters).astype(jnp.bfloat16) for det in range(whole.shape[0])]
    )


def per_device(strain, basis, recon):
    whole = lax.all_gather(strain, ("split", "shard"), axis=1, tiled=True)
    filters = basis[0]
    own_series = all_detectors(whole, filters)
    series = lax.all_gather(own_series, "shard", axis=1, tiled=True)
    weights = recon[0]
    detectors = series.shape[0]
    scale = 1.0 / (2.0 * detectors)
    templ = weights.shape[1]
    mblock = min(256, templ)
    blocks = []
    for mpos in range(templ // mblock):
        part = weights[:, mpos * mblock : (mpos + 1) * mblock]
        total = jnp.zeros((mblock, series.shape[2]), jnp.float32)
        for det in range(detectors):
            zvals = jnp.einsum("qml,lt->qmt", part, series[det], preferred_element_type=jnp.float32)
            total = total + jnp.sum(zvals * zvals, axis=0)
        blocks.append(total * scale)
    snr_local = jnp.concatenate(blocks, axis=0)
    loudest = lax.pmax(jnp.max(snr_local, axis=0), ("split", "shard"))
    return (snr_local[None], loudest)


def solution(mesh):
    return jax.shard_map(
        per_device,
        mesh=mesh,
        in_specs=(
            P(None, ("split", "shard")),
            P("split", "shard", None),
            P("split", None, "shard", None),
        ),
        out_specs=(P("split", "shard", None), P()),
        check_vma=False,
    )
```

profile of v0, /device:TPU:1, one launch (start us, length us, event | category | flops | bytes accessed | tf_op | source)
XLA Modules:
  0.0 618.8 jit_solution(15885630971313744312)
XLA Ops:
  7.2 303.4 %all-gather = bf16[128,32,3]{1,2,0:T(4,128)(2,1)S(1)} all-gather(bf16[1,32,3]{1,2,0:T(4,128)(2,1)} %bitcast.105), channel_id=1, replica_groups=mesh['split'=16,'shard'=8] {'split','shard'}, dimensions={0}, use_global_device_ids=true | all-gather | bytes 24768 | tf_op jit(solution)/shard_map/all_gather | solution.py:38
  315.4 1.8 reshape.429
  319.9 1.8 reshape.433
  327.3 2.0 reshape.436
  345.0 1.8 reshape.444
  352.6 1.9 fusion.144
  360.7 1.9 reshape.450
  364.5 2.2 fusion.153
  388.5 2.5 fusion.156
  395.9 2.3 fusion.162
  398.3 1.8 reshape.464
  402.2 2.1 fusion.165
  423.7 84.6 %all-gather.3.cloned.1.call-done = bf16[3,400,2048]{2,0,1:T(4,128)(2,1)} async-done(((bf16[3,50,2048]{2,0,1:T(4,128)(2,1)}), bf16[3,400,2048]{2,0,1:T(4,128)(2,1)}) %all-gather.3.cloned.1.call-update) | async-done | bytes 4915216 | tf_op jit(solution)/shard_map/all_gather | solution.py:41
  508.3 15.7 %fusion.202 = (bf16[1,400,2048]{2,0,1:T(2,128)(2,1)S(1)}, bf16[1,400,2048]{2,0,1:T(2,128)(2,1)S(1)}, bf16[1,400,2048]{2,0,1:T(2,128)(2,1)S(1)}) fusion(bf16[3,400,2048]{2,0,1:T(4,128)(2,1)} %all-gather.3.cloned.1.call-done), kind=kLoop, calls=%fused_computation.230 | loop fusion | bytes 9830400 | tf_op jit(solution)/shard_map/slice | solution.py:52
  524.0 2.0 multiply_reduce_fusion.1
  526.0 2.0 multiply_reduce_fusion.4
  528.0 2.0 multiply_reduce_fusion.2
  530.0 2.0 multiply_reduce_fusion.5
  532.0 2.0 multiply_reduce_fusion
  534.0 2.0 multiply_reduce_fusion.3
  536.0 1.9 fusion.198
  537.9 64.2 %pmax.7 = f32[2048]{0:T(1024)} all-reduce(f32[2048]{0:T(1024)S(1)} %reduce_max.19), channel_id=1, replica_groups=mesh['split'=16,'shard'=8] {'split','shard'}, use_global_device_ids=true, to_apply=%region_8.9 | all-reduce | flops 2048 | bytes 16384 | tf_op jit(solution)/shard_map/pmax | solution.py:56
  602.1 4.1 maximum_bitcast_fusion
  606.2 5.3 copy.11
  (236 shorter events, 89.6 us)
Async XLA Ops:
  7.2 345.4 %copy-start = (bf16[1,50,2048]{2,1,0:T(8,128)(2,1)S(1)}, bf16[1,50,2048]{2,1,0:T(8,128)(2,1)}, u32[]{:S(2)}) copy-start(bf16[1,50,2048]{2,1,0:T(8,128)(2,1)} %param.4) | copy-start | bytes 614404
  7.2 501.1 %all-gather.3.cloned.1.call-start = ((), (), s32[]{:S(2)}) async-start(), calls=%async_computation | async-start | bytes 7372800 | tf_op jit(solution)/shard_map/all_gather | solution.py:41
  362.5 2.0 copy-start.13
  364.5 2.2 copy-start.37
  364.5 2.2 copy-start.40
  368.5 2.8 copy-start.35
  368.5 2.8 copy-start.38
  373.1 2.8 copy-start.33
  373.1 2.7 copy-start.36
  377.6 2.8 copy-start.31
  377.7 2.8 copy-start.34
  388.4 2.5 copy-start.14
  388.5 2.5 copy-start.11
  388.5 2.5 copy-start.17
  395.8 2.3 copy-start.20
  395.9 2.3 copy-start.28
  400.2 2.0 copy-start.15
  402.1 2.2 copy-start.26
  406.1 1.9 copy-start.44
  410.8 2.8 copy-start.42
  410.8 2.8 copy-start.43
  415.4 2.0 slice-start
  415.4 2.0 copy-start.6
  423.7 100.3 %copy-start.46 = (bf16[1,2,512,400]{2,3,1,0:T(8,128)(2,1)S(1)}, bf16[1,2,512,400]{2,3,1,0:T(8,128)(2,1)}, u32[]{:S(2)}) copy-start(bf16[1,2,512,400]{2,3,1,0:T(8,128)(2,1)} %param.5) | copy-start | bytes 2457604
  (28 other events, 42.9 us)
Sparse Core Ops, SparseCore 0:
  423.8 84.4 all-gather.2
where the time goes:
time: 628 us; the launch traced here: 619 us
  blocking collectives  368 us (59%)
  local copies, waits for them, and re-layouts  115 us (18%)
  waiting for transfers between devices  84.6 us (13%)
  matrix products  29.4 us (5%)
  between operations  15.9 us (3%)
  other arithmetic  6.67 us (1%)
    all_gather x1, blocking collectives, per_device(): whole = lax.all_gather(strain, ('split', 'shard'), axis=1, tiled=True)  303 us
    all_gather x1, waiting for transfers between devices, per_device(): series = lax.all_gather(own_series, 'shard', axis=1, tiled=True)  84.6 us
    pmax x1, blocking collectives, per_device(): loudest = lax.pmax(jnp.max(snr_local, axis=0), ('split', 'shard'))  64.2 us
    reshape x21, local copies, waits for them, and re-layouts, toeplitz_block(): return flat.reshape(rows, width - 1)[:, :cols]  38.2 us
    reshape x21, local copies, waits for them, and re-layouts, toeplitz_block(): jnp.broadcast_to(turned, (rows, width)).reshape(-1)[:rows * (width - 1)]  35.8 us
    dot_general x12, matrix products, filter_series(): outputs.append(jnp.dot(filters, frame, preferred_element_type=jnp.float32))  17.4 us
    slice x1, local copies, waits for them, and re-layouts, per_device(): series[det]  15.7 us
  transfers between devices with their start and end apart: 1, of which 1 were waited for; matrix products, arithmetic and copies ran while one was open for 0% of the time, Pallas kernels for 0%

commit v1 on v0

v1 whole, which is shorter than its diff:
```python
import functools

import jax
import jax.numpy as jnp
from jax import lax
from jax.experimental import pallas as pl
from jax.experimental.pallas import tpu as pltpu
from jax.sharding import PartitionSpec as P

VMEM = pltpu.VMEM


def spread(block, axes, count):
    copies = jnp.broadcast_to(block[None], (count,) + block.shape)
    return lax.all_to_all(copies, axes, 0, 0, tiled=True)


def join_strain(parts_ref, det, piece):
    count = parts_ref.shape[0]
    part = parts_ref[:, det * piece : (det + 1) * piece].astype(jnp.float32)
    group = jnp.concatenate([part] * (128 // piece), axis=1)
    wide = jnp.concatenate([group] * (count * piece // 128), axis=1)
    owner = lax.broadcasted_iota(jnp.int32, wide.shape, 1) // piece
    mine = lax.broadcasted_iota(jnp.int32, wide.shape, 0)
    return jnp.sum(jnp.where(owner == mine, wide, 0.0), axis=0, keepdims=True)


def fill_slab(line, slab_ref, det):
    samples = line.shape[1]
    rows, cols = slab_ref.shape[1:]
    base = jnp.broadcast_to(line, (8, samples))
    first = pltpu.roll(base, samples - 7, 1, stride=1, stride_axis=0)
    turned = [first] + [pltpu.roll(first, samples - 8 * m, 1) for m in range(1, 16)]
    for m in range(1, 16, 2):
        pair = jnp.concatenate([turned[m], turned[m - 1]], axis=0).astype(jnp.bfloat16)
        for q in range(rows // 128):
            row = 16 * ((rows // 8 - 1 - 16 * q - m) // 2)
            slab_ref[det, row : row + 16, :] = pair[:, 128 * q : 128 * q + cols]


def bank_kernel(parts_ref, *refs, blocks, ndet, taps):
    block_refs = refs[:blocks]
    weights_ref, snr_ref, peak_ref, basis_ref, slab_ref, series_ref = refs[blocks:]
    step = pl.program_id(0)
    cols = slab_ref.shape[2]
    nbasis = basis_ref.shape[0]
    each = nbasis // blocks
    piece = parts_ref.shape[1] // ndet

    @pl.when(step == 0)
    def _():
        for det in range(ndet):
            fill_slab(join_strain(parts_ref, det, piece), slab_ref, det)
        for index in range(blocks):
            basis_ref[index * each : (index + 1) * each, :] = block_refs[index][...]
        series_ref[...] = jnp.zeros_like(series_ref)

    start = pl.multiple_of((pl.num_programs(0) - 1 - step) * cols, cols)
    templ = weights_ref.shape[0] // 2
    total = None
    for det in range(ndet):
        frame = slab_ref[det, pl.ds(start, taps), :]
        series = jnp.dot(basis_ref[...], frame, preferred_element_type=jnp.float32)
        series_ref[det, :nbasis, :] = series.astype(jnp.bfloat16)
        zvals = jnp.dot(weights_ref[...], series_ref[det], preferred_element_type=jnp.float32)
        power = zvals * zvals
        both = power[:templ] + power[templ:]
        total = both if total is None else total + both
    snr = total * (1.0 / (2.0 * ndet))
    snr_ref[...] = snr
    peak_ref[...] = jnp.max(snr, axis=0, keepdims=True)


def bank(parts, blocks, weights, ndet, cols):
    samples = parts.shape[0] * parts.shape[1] // ndet
    taps = blocks[0].shape[1]
    tout = samples - taps
    nbasis = sum(block.shape[0] for block in blocks)
    templ, depth = weights.shape[0] // 2, weights.shape[1]
    body = functools.partial(bank_kernel, blocks=len(blocks), ndet=ndet, taps=taps)
    flops = 2 * ndet * tout * (nbasis * taps + 2 * templ * nbasis)
    return pl.pallas_call(
        body,
        grid=(tout // cols,),
        in_specs=[pl.BlockSpec(memory_space=VMEM)] * (len(blocks) + 2),
        out_specs=[
            pl.BlockSpec((templ, cols), lambda i: (0, i)),
            pl.BlockSpec((1, cols), lambda i: (0, i)),
        ],
        out_shape=[
            jax.ShapeDtypeStruct((templ, tout), jnp.float32),
            jax.ShapeDtypeStruct((1, tout), jnp.float32),
        ],
        scratch_shapes=[
            VMEM((nbasis, taps), jnp.bfloat16),
            VMEM((ndet, samples - cols, cols), jnp.bfloat16),
            VMEM((ndet, depth, cols), jnp.bfloat16),
        ],
        compiler_params=pltpu.CompilerParams(vmem_limit_bytes=32 << 20),
        cost_estimate=pl.CostEstimate(
            flops=flops, bytes_accessed=4 * templ * tout + 2 * nbasis * taps, transcendentals=0
        ),
    )(parts, *blocks, weights)


def per_device(strain, basis, recon, nsplit, nshard):
    own = basis[0]
    ndet = strain.shape[0]
    each = own.shape[0]
    me = lax.axis_index("shard")

    blocks = [own]
    for away in range(1, nshard):
        pairs = [(i, i ^ away) for i in range(nshard)]
        blocks.append(lax.ppermute(own, "shard", pairs))
    parts = spread(strain.reshape(-1), ("split", "shard"), nsplit * nshard)

    nbasis = each * nshard
    depth = -(-nbasis // 256) * 256
    col = lax.broadcasted_iota(jnp.int32, (nbasis, depth), 1)
    source = ((col // each) ^ me) * each + col % each
    row = lax.broadcasted_iota(jnp.int32, (nbasis, depth), 0)
    order = ((row == source) & (col < nbasis)).astype(jnp.bfloat16)
    weights = jnp.einsum("qml,lp->qmp", recon[0], order, preferred_element_type=jnp.float32)
    weights = weights.astype(jnp.bfloat16).reshape(-1, depth)

    snr, peak = bank(parts, blocks, weights, ndet, 512)

    peak = peak.reshape(-1)
    peak = jnp.max(spread(peak, "shard", nshard), axis=0)
    loudest = jnp.max(spread(peak, "split", nsplit), axis=0)
    return (snr[None], loudest)


def solution(mesh):
    body = functools.partial(
        per_device, nsplit=mesh.shape["split"], nshard=mesh.shape["shard"]
    )
    return jax.shard_map(
        body,
        mesh=mesh,
        in_specs=(
            P(None, ("split", "shard")),
            P("split", "shard", None),
            P("split", None, "shard", None),
        ),
        out_specs=(P("split", "shard", None), P()),
        check_vma=False,
    )
```

time: 628 us -> 84.7 us (0.13); the launches traced: 619 us -> 84.5 us
  blocking collectives: 368 us -> 24.7 us
  local copies, waits for them, and re-layouts: 115 us -> 2.78 us
  waiting for transfers between devices: 84.6 us -> 9.24 us
  matrix products: 29.4 us -> 1.79 us
  starting transfers between devices: 0.04 us -> 22.5 us
  Pallas kernels: 0 us -> 22 us
  between operations: 15.9 us -> 0.73 us
    all_gather x1 -> x0, blocking collectives: 303 us -> none  [per_device(): whole = lax.all_gather(strain, ('split', 'shard'), axis=1, tiled=True)]
    all_gather x1 -> x0, waiting for transfers between devices: 84.6 us -> none  [per_device(): series = lax.all_gather(own_series, 'shard', axis=1, tiled=True)]
    reshape x42 -> x0, local copies, waits for them, and re-layouts: 74 us -> none  [the longest x21 38.2 us: toeplitz_block(): return flat.reshape(rows, width - 1)[:, :cols]]
    pmax x1 -> x0, blocking collectives: 64.2 us -> none  [per_device(): loudest = lax.pmax(jnp.max(snr_local, axis=0), ('split', 'shard'))]
    slice x51 -> x0, local copies, waits for them, and re-layouts: 29.1 us -> none  [the longest x1 15.7 us: per_device(): series[det]]
    dot_general x18 -> x1, matrix products: 29.4 us -> 1.79 us  [per_device(): jnp.einsum('qml,lp->qmp', recon[0], order, preferred_element_type=jnp.flo...]
    all_to_all x0 -> x2, blocking collectives: none -> 24.7 us  [spread(): return lax.all_to_all(copies, axes, 0, 0, tiled=True)]
    pallas_call x0 -> x1, Pallas kernels: none -> 22 us  [bank(): pl.pallas_call(body, grid=(tout // cols,), in_specs=[pl.BlockSpec(memory_...]
  transfers between devices with their start and end apart: 1 -> 8, of which waited for: 1 -> 2; matrix products, arithmetic and copies ran while one was open for 0% -> 4% of each run, Pallas kernels for 0% -> 0%
where the time goes in v1:
time: 84.7 us; the launch traced here: 84.5 us
  blocking collectives  24.7 us (29%)
  starting transfers between devices  22.5 us (27%)
  Pallas kernels  22 us (26%)
  waiting for transfers between devices  9.24 us (11%)
  local copies, waits for them, and re-layouts  2.78 us (3%)
  matrix products  1.79 us (2%)
    all_to_all x2, blocking collectives, spread(): return lax.all_to_all(copies, axes, 0, 0, tiled=True)  24.7 us
    pallas_call x1, Pallas kernels, bank(): pl.pallas_call(body, grid=(tout // cols,), in_specs=[pl.BlockSpec(memory_...  22 us
    ppermute x7, starting transfers between devices, per_device(): blocks.append(lax.ppermute(own, 'shard', pairs))  13.9 us
    all_to_all x1, starting transfers between devices, spread(): return lax.all_to_all(copies, axes, 0, 0, tiled=True)  8.59 us
    ppermute x7, waiting for transfers between devices, per_device(): blocks.append(lax.ppermute(own, 'shard', pairs))  5.03 us
    all_to_all x1, waiting for transfers between devices, spread(): return lax.all_to_all(copies, axes, 0, 0, tiled=True)  4.2 us
    dot_general x1, matrix products, per_device(): jnp.einsum('qml,lp->qmp', recon[0], order, preferred_element_type=jnp.flo...  1.79 us
  transfers between devices with their start and end apart: 8, of which 2 were waited for; matrix products, arithmetic and copies ran while one was open for 4% of the time, Pallas kernels for 0%

profile of v1, /device:TPU:1, one launch (start us, length us, event | category | flops | bytes accessed | tf_op | source)
XLA Modules:
  0.0 84.5 jit_solution(6274780090117744635)
XLA Ops:
  0.6 0.0 copy-start
  0.6 0.0 copy-start.1
  0.7 5.7 %collective-permute-start.6 = (bf16[50,2048]{1,0:T(8,128)(2,1)}, bf16[50,2048]{1,0:T(8,128)(2,1)S(1)}, u32[]{:S(2)}, u32[]{:S(2)}) collective-permute-start(bf16[50,2048]{1,0:T(8,128)(2,1)} %bitcast.18), channel_id=1, source_target_pairs={{0,7},{1,6},{2,5},{3,4},{4,3},{5,2},{6,1},{7,0},{8,15},{9,14},{10,... | collective-permute-start | bytes 614408 | tf_op jit(solution)/shard_map/ppermute | solution.py:115
  6.3 0.0 collective-permute-start.5
  6.3 0.6 collective-permute-start.4
  6.9 1.3 %collective-permute-start.3 = (bf16[50,2048]{1,0:T(8,128)(2,1)}, bf16[50,2048]{1,0:T(8,128)(2,1)S(1)}, u32[]{:S(2)}, u32[]{:S(2)}) collective-permute-start(bf16[50,2048]{1,0:T(8,128)(2,1)} %bitcast.21), channel_id=1, source_target_pairs={{0,4},{1,5},{2,6},{3,7},{4,0},{5,1},{6,2},{7,3},{8,12},{9,13},{10,... | collective-permute-start | bytes 614408 | tf_op jit(solution)/shard_map/ppermute | solution.py:115
  8.2 2.5 %collective-permute-start.2 = (bf16[50,2048]{1,0:T(8,128)(2,1)}, bf16[50,2048]{1,0:T(8,128)(2,1)S(1)}, u32[]{:S(2)}, u32[]{:S(2)}) collective-permute-start(bf16[50,2048]{1,0:T(8,128)(2,1)} %bitcast.22), channel_id=1, source_target_pairs={{0,3},{1,2},{2,1},{3,0},{4,7},{5,6},{6,5},{7,4},{8,11},{9,10},{10,... | collective-permute-start | bytes 614408 | tf_op jit(solution)/shard_map/ppermute | solution.py:115
  10.7 0.8 broadcast_in_dim.10
  11.4 0.7 broadcast_in_dim.22
  12.1 8.6 %all-to-all-start = ((bf16[128,1,96]{2,1,0:T(2,128)(2,1)}), bf16[128,1,96]{2,1,0:T(2,128)(2,1)S(1)}, u32[]{:S(2)}, u32[]{:S(2)}) async-start(bf16[128,1,96]{2,1,0:T(2,128)(2,1)} %broadcast_in_dim.22), calls=%async_computation | async-start | bytes 131072 | tf_op jit(solution)/shard_map/all_to_all | solution.py:15
  20.7 0.0 collective-permute-done.6.refs_7_
  20.8 3.4 %collective-permute-start.1 = (bf16[50,2048]{1,0:T(8,128)(2,1)}, bf16[50,2048]{1,0:T(8,128)(2,1)S(1)}, u32[]{:S(2)}, u32[]{:S(2)}) collective-permute-start(bf16[50,2048]{1,0:T(8,128)(2,1)} %bitcast.23), channel_id=1, source_target_pairs={{0,2},{1,3},{2,0},{3,1},{4,6},{5,7},{6,4},{7,5},{8,10},{9,11},{10,... | collective-permute-start | bytes 614408 | tf_op jit(solution)/shard_map/ppermute | solution.py:115
  24.1 0.6 collective-permute-start
  24.7 1.8 %convolution_convert_fusion = bf16[512,2,512]{0,2,1:T(8,128)(2,1)} fusion(bf16[1,2,512,400]{2,3,1,0:T(8,128)(2,1)S(1)} %copy-done, s32[512]{0:T(512)S(1)} %get-tuple-element.7, s32[512]{0:T(512)S(1)} %get-tuple-element.8, s32[]{:T(128)S(6)} %axis_index.12, s32[512]{0:T(512)S(1)} %get-tuple-element.6, s32[512]{0:T(512)S(1)} %get-tuple-element.9, ...), kind=kOutput, calls=%fused_computation | convolution fusion | flops 421388288 | bytes 1877508 | tf_op jit(solution)/shard_map/qml,lp->qmp/dot_general | solution.py:124
  26.5 4.2 %all-to-all-done = bf16[128,1,96]{2,1,0:T(2,128)(2,1)S(1)} async-done(((bf16[128,1,96]{2,1,0:T(2,128)(2,1)}), bf16[128,1,96]{2,1,0:T(2,128)(2,1)S(1)}, u32[]{:S(2)}, u32[]{:S(2)}) %all-to-all-start) | async-done | bytes 24608 | tf_op jit(solution)/shard_map/all_to_all | solution.py:15
  30.7 0.0 collective-permute-done.4.refs_5_
  30.7 5.0 %collective-permute-done.refs_1_ = bf16[50,2048]{1,0:T(8,128)(2,1)S(1)} collective-permute-done((bf16[50,2048]{1,0:T(8,128)(2,1)}, bf16[50,2048]{1,0:T(8,128)(2,1)S(1)}, u32[]{:S(2)}, u32[]{:S(2)}) %collective-permute-start) | collective-permute-done | bytes 204832 | tf_op jit(solution)/shard_map/ppermute | solution.py:115
  35.7 1.2 %copy-done.2 = bf16[512,2,512]{0,2,1:T(8,128)(2,1)S(1)} copy-done((bf16[512,2,512]{0,2,1:T(8,128)(2,1)S(1)}, bf16[512,2,512]{0,2,1:T(8,128)(2,1)}, u32[]{:S(2)}) %copy-start.2) | copy-done | bytes 1048600
  37.0 22.0 %shard_map.50 = (f32[512,2048]{1,0:T(8,128)}, f32[1,2048]{1,0:T(1,128)S(1)}) custom-call(bf16[128,96]{1,0:T(8,128)(2,1)S(1)} %bitcast.16, bf16[50,2048]{1,0:T(8,128)(2,1)S(1)} %bitcast.25, bf16[50,2048]{1,0:T(8,128)(2,1)S(1)} %collective-permute-done.refs_1_, bf16[50,2048]{1,0:T(8,128)(2,1)S(1)} %collective-permute-done.1.refs_2_, ...), custom_call_target="tpu_custom_call" | custom-call | flops 15099494400 | bytes 5832704 | tf_op jit(solution)/shard_map/pallas_call | solution.py:82
  58.9 8.6 %all_to_all.20 = f32[8,1,2048]{2,1,0:T(1,128)S(1)} all-to-all(f32[8,1,2048]{2,1,0:T(1,128)S(1)} %broadcast_in_dim.24), channel_id=1, replica_groups=mesh['split'=16,'shard'=8] {'shard'}, dimensions={0} | all-to-all | bytes 131072 | tf_op jit(solution)/shard_map/all_to_all | solution.py:15
  67.5 0.1 reduce_max.18
  67.6 0.1 broadcast_in_dim.25
  67.6 16.1 %all_to_all.21 = f32[16,1,2048]{2,1,0:T(1,128)S(1)} all-to-all(f32[16,1,2048]{2,1,0:T(1,128)S(1)} %broadcast_in_dim.25), channel_id=1, replica_groups=mesh['split'=16,'shard'=8] {'split'}, dimensions={0} | all-to-all | bytes 262144 | tf_op jit(solution)/shard_map/all_to_all | solution.py:15
  83.8 0.7 reduce_max.19
  (13 shorter events, 0.1 us)
Async XLA Ops:
  0.6 24.0 %copy-start = (bf16[1,2,512,400]{2,3,1,0:T(8,128)(2,1)S(1)}, bf16[1,2,512,400]{2,3,1,0:T(8,128)(2,1)}, u32[]{:S(2)}) copy-start(bf16[1,2,512,400]{2,3,1,0:T(8,128)(2,1)} %param.5) | copy-start | bytes 2457604
  0.6 35.1 %copy-start.1 = (bf16[1,50,2048]{2,1,0:T(8,128)(2,1)S(1)}, bf16[1,50,2048]{2,1,0:T(8,128)(2,1)}, u32[]{:S(2)}) copy-start(bf16[1,50,2048]{2,1,0:T(8,128)(2,1)} %param.4) | copy-start | bytes 614404
  0.7 20.1 %collective-permute-start.6 = (bf16[50,2048]{1,0:T(8,128)(2,1)}, bf16[50,2048]{1,0:T(8,128)(2,1)S(1)}, u32[]{:S(2)}, u32[]{:S(2)}) collective-permute-start(bf16[50,2048]{1,0:T(8,128)(2,1)} %bitcast.18), channel_id=1, source_target_pairs={{0,7},{1,6},{2,5},{3,4},{4,3},{5,2},{6,1},{7,0},{8,15},{9,14},{10,... | collective-permute-start | bytes 614408 | tf_op jit(solution)/shard_map/ppermute | solution.py:115
  6.3 17.8 %collective-permute-start.5 = (bf16[50,2048]{1,0:T(8,128)(2,1)}, bf16[50,2048]{1,0:T(8,128)(2,1)S(1)}, u32[]{:S(2)}, u32[]{:S(2)}) collective-permute-start(bf16[50,2048]{1,0:T(8,128)(2,1)} %bitcast.19), channel_id=1, source_target_pairs={{0,6},{1,7},{2,4},{3,5},{4,2},{5,3},{6,0},{7,1},{8,14},{9,15},{10,... | collective-permute-start | bytes 614408 | tf_op jit(solution)/shard_map/ppermute | solution.py:115
  6.3 24.3 %collective-permute-start.4 = (bf16[50,2048]{1,0:T(8,128)(2,1)}, bf16[50,2048]{1,0:T(8,128)(2,1)S(1)}, u32[]{:S(2)}, u32[]{:S(2)}) collective-permute-start(bf16[50,2048]{1,0:T(8,128)(2,1)} %bitcast.20), channel_id=1, source_target_pairs={{0,5},{1,4},{2,7},{3,6},{4,1},{5,0},{6,3},{7,2},{8,13},{9,12},{10,... | collective-permute-start | bytes 614408 | tf_op jit(solution)/shard_map/ppermute | solution.py:115
  6.9 23.8 %collective-permute-start.3 = (bf16[50,2048]{1,0:T(8,128)(2,1)}, bf16[50,2048]{1,0:T(8,128)(2,1)S(1)}, u32[]{:S(2)}, u32[]{:S(2)}) collective-permute-start(bf16[50,2048]{1,0:T(8,128)(2,1)} %bitcast.21), channel_id=1, source_target_pairs={{0,4},{1,5},{2,6},{3,7},{4,0},{5,1},{6,2},{7,3},{8,12},{9,13},{10,... | collective-permute-start | bytes 614408 | tf_op jit(solution)/shard_map/ppermute | solution.py:115
  8.2 22.5 %collective-permute-start.2 = (bf16[50,2048]{1,0:T(8,128)(2,1)}, bf16[50,2048]{1,0:T(8,128)(2,1)S(1)}, u32[]{:S(2)}, u32[]{:S(2)}) collective-permute-start(bf16[50,2048]{1,0:T(8,128)(2,1)} %bitcast.22), channel_id=1, source_target_pairs={{0,3},{1,2},{2,1},{3,0},{4,7},{5,6},{6,5},{7,4},{8,11},{9,10},{10,... | collective-permute-start | bytes 614408 | tf_op jit(solution)/shard_map/ppermute | solution.py:115
  12.1 18.6 %all-to-all-start = ((bf16[128,1,96]{2,1,0:T(2,128)(2,1)}), bf16[128,1,96]{2,1,0:T(2,128)(2,1)S(1)}, u32[]{:S(2)}, u32[]{:S(2)}) async-start(bf16[128,1,96]{2,1,0:T(2,128)(2,1)} %broadcast_in_dim.22), calls=%async_computation | async-start | bytes 131072 | tf_op jit(solution)/shard_map/all_to_all | solution.py:15
  20.8 9.9 %collective-permute-start.1 = (bf16[50,2048]{1,0:T(8,128)(2,1)}, bf16[50,2048]{1,0:T(8,128)(2,1)S(1)}, u32[]{:S(2)}, u32[]{:S(2)}) collective-permute-start(bf16[50,2048]{1,0:T(8,128)(2,1)} %bitcast.23), channel_id=1, source_target_pairs={{0,2},{1,3},{2,0},{3,1},{4,6},{5,7},{6,4},{7,5},{8,10},{9,11},{10,... | collective-permute-start | bytes 614408 | tf_op jit(solution)/shard_map/ppermute | solution.py:115
  24.1 11.6 %collective-permute-start = (bf16[50,2048]{1,0:T(8,128)(2,1)}, bf16[50,2048]{1,0:T(8,128)(2,1)S(1)}, u32[]{:S(2)}, u32[]{:S(2)}) collective-permute-start(bf16[50,2048]{1,0:T(8,128)(2,1)} %bitcast.24), channel_id=1, source_target_pairs={{0,1},{1,0},{2,3},{3,2},{4,5},{5,4},{6,7},{7,6},{8,9},{9,8},{10,11... | collective-permute-start | bytes 614408 | tf_op jit(solution)/shard_map/ppermute | solution.py:115
  35.7 1.2 %copy-start.2 = (bf16[512,2,512]{0,2,1:T(8,128)(2,1)S(1)}, bf16[512,2,512]{0,2,1:T(8,128)(2,1)}, u32[]{:S(2)}) copy-start(bf16[512,2,512]{0,2,1:T(8,128)(2,1)} %convolution_convert_fusion) | copy-start | bytes 3145732

commit v2 on v1

v2 whole, which is shorter than its diff:
```python
import functools

import jax
import jax.numpy as jnp
from jax import lax
from jax.experimental import pallas as pl
from jax.experimental.pallas import tpu as pltpu
from jax.sharding import PartitionSpec as P

VMEM = pltpu.VMEM
LIMIT = 30 << 20
COLS = 512
EARLY = 4


def spread(block, axes, count):
    copies = jnp.broadcast_to(block[None], (count,) + block.shape)
    return lax.all_to_all(copies, axes, 0, 0, tiled=True)


def join_strain(parts_ref, lines_ref, turned_ref):
    ndet = lines_ref.shape[0]
    count, piece = parts_ref.shape[0], parts_ref.shape[1] // ndet
    side = 128 // piece
    rows = count // side
    for det in range(ndet):
        cut = slice(det * piece, (det + 1) * piece)
        quarters = [parts_ref[pl.ds(j, rows, stride=side), :][:, cut] for j in range(side)]
        turned_ref[...] = jnp.concatenate(quarters, axis=1)
        for row in range(rows):
            lines_ref[det : det + 1, 128 * row : 128 * row + 128] = turned_ref[row : row + 1, :]


def fill_slab(line, slab_ref, det):
    samples = line.shape[1]
    rows, cols = slab_ref.shape[1:]
    base = jnp.broadcast_to(line, (8, samples))
    first = pltpu.roll(base, samples - 7, 1, stride=1, stride_axis=0)
    turned = [first] + [pltpu.roll(first, samples - 8 * m, 1) for m in range(1, 16)]
    for m in range(1, 16, 2):
        pair = jnp.concatenate([turned[m], turned[m - 1]], axis=0).astype(jnp.bfloat16)
        for q in range(rows // 128):
            row = 16 * ((rows // 8 - 1 - 16 * q - m) // 2)
            slab_ref[det, row : row + 16, :] = pair[:, 128 * q : 128 * q + cols]


def prepare(lines_ref, block_refs, slab_ref, basis_ref):
    for det in range(slab_ref.shape[0]):
        fill_slab(lines_ref[det : det + 1, :], slab_ref, det)
    row = 0
    for block_ref in block_refs:
        each = block_ref.shape[0]
        basis_ref[row : row + each, :] = block_ref[...]
        row += each


def filtered(basis_ref, slab_ref, det, step, steps):
    taps, cols = basis_ref.shape[1], slab_ref.shape[2]
    start = pl.multiple_of((steps - 1 - step) * cols, cols)
    frame = slab_ref[det, pl.ds(start, taps), :]
    return jnp.dot(basis_ref[...], frame, preferred_element_type=jnp.float32).astype(jnp.bfloat16)


def early_kernel(parts_ref, *refs, blocks):
    block_refs = refs[:blocks]
    out_ref, lines_ref, basis_ref, slab_ref, turned_ref = refs[blocks:]
    step = pl.program_id(0)

    @pl.when(step == 0)
    def _():
        join_strain(parts_ref, lines_ref, turned_ref)
        prepare(lines_ref, block_refs, slab_ref, basis_ref)

    for det in range(out_ref.shape[0]):
        out_ref[det] = filtered(basis_ref, slab_ref, det, step, pl.num_programs(0))


def late_kernel(lines_ref, early_ref, weights_ref, *refs, blocks):
    block_refs = refs[:blocks]
    snr_ref, peak_ref, basis_ref, slab_ref, series_ref = refs[blocks:]
    step, steps = pl.program_id(0), pl.num_programs(0)
    ndet, nearly = early_ref.shape[:2]
    nlate = basis_ref.shape[0]

    @pl.when(step == 0)
    def _():
        prepare(lines_ref, block_refs, slab_ref, basis_ref)
        series_ref[...] = jnp.zeros_like(series_ref)

    templ = weights_ref.shape[0] // 2

    def fill(det):
        series_ref[det, :nearly, :] = early_ref[det]
        late = filtered(basis_ref, slab_ref, det, step, steps)
        series_ref[det, nearly : nearly + nlate, :] = late

    total = None
    fill(0)
    for det in range(ndet):
        if det + 1 < ndet:
            fill(det + 1)
        zvals = jnp.dot(weights_ref[...], series_ref[det], preferred_element_type=jnp.float32)
        power = zvals * zvals
        both = power[:templ] + power[templ:]
        total = both if total is None else total + both
    snr = total * (1.0 / (2.0 * ndet))
    snr_ref[...] = snr
    peak_ref[...] = jnp.max(snr, axis=0, keepdims=True)


def early_series(parts, blocks, ndet):
    samples = parts.size // ndet
    taps = blocks[0].shape[1]
    tout = samples - taps
    nearly = sum(block.shape[0] for block in blocks)
    return pl.pallas_call(
        functools.partial(early_kernel, blocks=len(blocks)),
        grid=(tout // COLS,),
        in_specs=[pl.BlockSpec(memory_space=VMEM)] * (len(blocks) + 1),
        out_specs=[
            pl.BlockSpec((ndet, nearly, COLS), lambda i: (0, 0, i)),
            pl.BlockSpec((ndet, samples), lambda i: (0, 0)),
        ],
        out_shape=[
            jax.ShapeDtypeStruct((ndet, nearly, tout), jnp.bfloat16),
            jax.ShapeDtypeStruct((ndet, samples), jnp.float32),
        ],
        scratch_shapes=[
            VMEM((nearly, taps), jnp.bfloat16),
            VMEM((ndet, samples - COLS, COLS), jnp.bfloat16),
            VMEM((samples // 128, 128), jnp.float32),
        ],
        compiler_params=pltpu.CompilerParams(vmem_limit_bytes=LIMIT),
    )(parts, *blocks)


def bank(lines, early, blocks, weights):
    ndet, nearly, tout = early.shape
    taps = blocks[0].shape[1]
    samples = tout + taps
    nlate = sum(block.shape[0] for block in blocks)
    templ, depth = weights.shape[0] // 2, weights.shape[1]
    steps = tout // COLS
    whole = pl.BlockSpec(memory_space=VMEM)
    return pl.pallas_call(
        functools.partial(late_kernel, blocks=len(blocks)),
        grid=(steps,),
        in_specs=[whole, pl.BlockSpec((ndet, nearly, COLS), lambda i: (0, 0, i)), whole]
        + [whole] * len(blocks),
        out_specs=[
            pl.BlockSpec((templ, COLS), lambda i: (0, i)),
            pl.BlockSpec((1, COLS), lambda i: (0, i)),
        ],
        out_shape=[
            jax.ShapeDtypeStruct((templ, tout), jnp.float32),
            jax.ShapeDtypeStruct((1, tout), jnp.float32),
        ],
        scratch_shapes=[
            VMEM((nlate, taps), jnp.bfloat16),
            VMEM((ndet, samples - COLS, COLS), jnp.bfloat16),
            VMEM((ndet, depth, COLS), jnp.bfloat16),
        ],
        compiler_params=pltpu.CompilerParams(vmem_limit_bytes=LIMIT),
    )(lines, early, weights, *blocks)


def per_device(strain, basis, recon, nsplit, nshard):
    own = basis[0]
    each = own.shape[0]
    count = nsplit * nshard
    me = lax.axis_index("shard")

    parts = spread(strain.astype(jnp.float32).reshape(-1), ("split", "shard"), count)

    def swap(block, away):
        pairs = [(i, i ^ away) for i in range(nshard)]
        return lax.ppermute(block, "shard", pairs)

    got = {0: own}
    for away in (4, 1, 3, 2):
        got[away] = swap(own, away)
    got[5] = swap(got[4], 1)
    got[7] = swap(got[4], 3)
    got[6] = swap(got[2], 4)
    far = [0, 4, 1, 3, 2, 5, 7, 6]
    blocks = [got[away] for away in far]

    nbasis = each * nshard
    depth = -(-nbasis // 256) * 256
    col = lax.broadcasted_iota(jnp.int32, (nbasis, depth), 1)
    row = lax.broadcasted_iota(jnp.int32, (nbasis, depth), 0)
    away = jnp.zeros((nbasis, depth), jnp.int32)
    for place, distance in enumerate(far):
        away = jnp.where(col // each == place, distance, away)
    source = (away ^ me) * each + col % each
    order = ((row == source) & (col < nbasis)).astype(jnp.bfloat16)
    weights = jnp.einsum("qml,lp->qmp", recon[0], order, preferred_element_type=jnp.float32)
    weights = weights.astype(jnp.bfloat16).reshape(-1, depth)

    early, lines = early_series(parts, blocks[:EARLY], strain.shape[0])
    snr, peak = bank(lines, early, blocks[EARLY:], weights)

    peak = jnp.max(spread(peak.reshape(-1), "shard", nshard), axis=0)
    loudest = jnp.max(spread(peak, "split", nsplit), axis=0)
    return (snr[None], loudest)


def solution(mesh):
    body = functools.partial(
        per_device, nsplit=mesh.shape["split"], nshard=mesh.shape["shard"]
    )
    return jax.shard_map(
        body,
        mesh=mesh,
        in_specs=(
            P(None, ("split", "shard")),
            P("split", "shard", None),
            P("split", None, "shard", None),
        ),
        out_specs=(P("split", "shard", None), P()),
        check_vma=False,
    )
```

time: 84.7 us -> 75.2 us (0.89)
  waiting for transfers between devices: 9.24 us -> 4.32 us
  blocking collectives: 24.7 us -> 20.8 us
  Pallas kernels: 22 us -> 23.9 us
  local copies, waits for them, and re-layouts: 2.78 us -> 1.54 us
  matrix products: 1.79 us -> 0.82 us
    ppermute x7, waiting for transfers between devices: 5.03 us -> 0.02 us  [swap(): return lax.ppermute(block, 'shard', pairs)]
    all_to_all x2, blocking collectives: 24.7 us -> 20.8 us  [spread(): return lax.all_to_all(copies, axes, 0, 0, tiled=True)]
    ppermute x7, starting transfers between devices: 13.9 us -> 11.1 us  [swap(): return lax.ppermute(block, 'shard', pairs)]
    all_to_all x1, starting transfers between devices: 8.59 us -> 10.9 us  [spread(): return lax.all_to_all(copies, axes, 0, 0, tiled=True)]
    pallas_call x1 -> x2, Pallas kernels: 22 us -> 23.9 us  [the longest x1 16.4 us: bank(): pl.pallas_call(functools.partial(late_kernel, blocks=len(blocks)), grid=(...]
    unnamed x6 -> x4, local copies, waits for them, and re-layouts: 1.24 us -> 0.01 us
    dot_general x1, matrix products: 1.79 us -> 0.82 us  [per_device(): jnp.einsum('qml,lp->qmp', recon[0], order, preferred_element_type=jnp.flo...]
  transfers between devices with their start and end apart: 8 -> 8, of which waited for: 2 -> 1; matrix products, arithmetic and copies ran while one was open for 4% -> 3% of each run, Pallas kernels for 0% -> 10%
where the time goes in v2:
time: 75.2 us; the launch traced here: 74.9 us
  Pallas kernels  23.9 us (32%)
  starting transfers between devices  22 us (29%)
  blocking collectives  20.8 us (28%)
  waiting for transfers between devices  4.32 us (6%)
  local copies, waits for them, and re-layouts  1.54 us (2%)
  matrix products  0.82 us (1%)
  other arithmetic  0.78 us (1%)
    all_to_all x2, blocking collectives, spread(): return lax.all_to_all(copies, axes, 0, 0, tiled=True)  20.8 us
    pallas_call x1, Pallas kernels, bank(): pl.pallas_call(functools.partial(late_kernel, blocks=len(blocks)), grid=(...  16.4 us
    ppermute x7, starting transfers between devices, swap(): return lax.ppermute(block, 'shard', pairs)  11.1 us
    all_to_all x1, starting transfers between devices, spread(): return lax.all_to_all(copies, axes, 0, 0, tiled=True)  10.9 us
    pallas_call x1, Pallas kernels, early_series(): pl.pallas_call(functools.partial(early_kernel, blocks=len(blocks)), grid=...  7.45 us
    all_to_all x1, waiting for transfers between devices, spread(): return lax.all_to_all(copies, axes, 0, 0, tiled=True)  4.3 us
    broadcast_in_dim x4, local copies, waits for them, and re-layouts, spread(): copies = jnp.broadcast_to(block[None], (count,) + block.shape)  1.53 us
  transfers between devices with their start and end apart: 8, of which 1 were waited for; matrix products, arithmetic and copies ran while one was open for 3% of the time, Pallas kernels for 10%

profile of v2, /device:TPU:1, one launch (start us, length us, event | category | flops | bytes accessed | tf_op | source)
XLA Modules:
  0.0 74.9 jit_solution(17374080402285876854)
XLA Ops:
  0.6 0.0 copy-start
  0.6 4.5 %collective-permute-start.3 = (bf16[50,2048]{1,0:T(8,128)(2,1)}, bf16[50,2048]{1,0:T(8,128)(2,1)S(1)}, u32[]{:S(2)}, u32[]{:S(2)}) collective-permute-start(bf16[50,2048]{1,0:T(8,128)(2,1)} %bitcast.15), channel_id=1, source_target_pairs={{0,2},{1,3},{2,0},{3,1},{4,6},{5,7},{6,4},{7,5},{8,10},{9,11},{10,... | collective-permute-start | bytes 614408 | tf_op jit(solution)/shard_map/ppermute | solution.py:177
  5.2 0.4 collective-permute-start.2
  5.6 0.3 collective-permute-start.1
  5.9 1.3 %collective-permute-start = (bf16[50,2048]{1,0:T(8,128)(2,1)}, bf16[50,2048]{1,0:T(8,128)(2,1)S(1)}, u32[]{:S(2)}, u32[]{:S(2)}) collective-permute-start(bf16[50,2048]{1,0:T(8,128)(2,1)} %bitcast.18), channel_id=1, source_target_pairs={{0,4},{1,5},{2,6},{3,7},{4,0},{5,1},{6,2},{7,3},{8,12},{9,13},{10,... | collective-permute-start | bytes 614408 | tf_op jit(solution)/shard_map/ppermute | solution.py:177
  7.2 0.8 %reshape.29 = f32[96]{0:T(128)S(1)} reshape(bf16[3,32]{1,0:T(4,128)(2,1)} %param.3) | data formatting | bytes 576 | tf_op jit(solution)/shard_map/broadcast_in_dim | solution.py:17
  7.9 0.7 broadcast_in_dim.38
  8.6 10.9 %all-to-all-start = ((f32[128,1,96]{2,1,0:T(1,128)}), f32[128,1,96]{2,1,0:T(1,128)S(1)}, u32[]{:S(2)}, u32[]{:S(2)}) async-start(f32[128,1,96]{2,1,0:T(1,128)} %broadcast_in_dim.38), calls=%async_computation | async-start | bytes 131072 | tf_op jit(solution)/shard_map/all_to_all | solution.py:18
  19.5 0.0 collective-permute-done.refs_1_
  19.5 3.3 %collective-permute-start.5 = (bf16[50,2048]{1,0:T(8,128)(2,1)S(1)}, bf16[50,2048]{1,0:T(8,128)(2,1)S(1)}, u32[]{:S(2)}, u32[]{:S(2)}) collective-permute-start(bf16[50,2048]{1,0:T(8,128)(2,1)S(1)} %collective-permute-done.refs_1_), channel_id=1, source_target_pairs={{0,3},{1,2},{2,1},{3,0},{4,7},{5,6},{6,5},{7,4},{8,11},{9,10},{10,... | collective-permute-start | bytes 614408 | tf_op jit(solution)/shard_map/ppermute | solution.py:177
  22.9 0.0 collective-permute-start.4
  22.9 0.0 collective-permute-done.3.refs_0_
  22.9 1.3 %collective-permute-start.6 = (bf16[50,2048]{1,0:T(8,128)(2,1)S(1)}, bf16[50,2048]{1,0:T(8,128)(2,1)}, u32[]{:S(2)}, u32[]{:S(2)}) collective-permute-start(bf16[50,2048]{1,0:T(8,128)(2,1)S(1)} %collective-permute-done.3.refs_0_), channel_id=1, source_target_pairs={{0,4},{1,5},{2,6},{3,7},{4,0},{5,1},{6,2},{7,3},{8,12},{9,13},{10,... | collective-permute-start | bytes 614408 | tf_op jit(solution)/shard_map/ppermute | solution.py:177
  24.1 0.8 %convolution_convert_fusion = bf16[512,2,512]{0,2,1:T(8,128)(2,1)S(1)} fusion(bf16[1,2,512,400]{2,3,1,0:T(8,128)(2,1)S(1)} %copy-done, s32[512]{0:T(512)S(1)} %get-tuple-element.11, s32[512]{0:T(512)S(1)} %get-tuple-element.12, s32[]{:T(128)S(6)} %axis_index.12, s32[512]{0:T(512)S(1)} %get-tuple-element.10, s32[512]{0:T(512)S(1)} %get-tuple-element.13, ...), kind=kOutput, calls=%fused_computation.7 | convolution fusion | flops 424255488 | bytes 1877508 | tf_op jit(solution)/shard_map/qml,lp->qmp/dot_general | solution.py:197
  25.0 4.3 %all-to-all-done = f32[128,1,96]{2,1,0:T(1,128)S(1)} async-done(((f32[128,1,96]{2,1,0:T(1,128)}), f32[128,1,96]{2,1,0:T(1,128)S(1)}, u32[]{:S(2)}, u32[]{:S(2)}) %all-to-all-start) | async-done | bytes 49184 | tf_op jit(solution)/shard_map/all_to_all | solution.py:18
  29.3 0.0 collective-permute-done.2.refs_3_
  29.3 7.5 %shard_map.50 = (bf16[3,200,2048]{2,1,0:T(8,128)(2,1)S(1)}, f32[3,4096]{1,0:T(4,128)S(1)}) custom-call(f32[128,96]{1,0:T(8,128)S(1)} %bitcast.14, bf16[50,2048]{1,0:T(8,128)(2,1)S(1)} %bitcast.19, bf16[50,2048]{1,0:T(8,128)(2,1)S(1)} %collective-permute-done.refs_1_, bf16[50,2048]{1,0:T(8,128)(2,1)S(1)} %collective-permute-done.1.refs_2_, ...), custom_call_target="tpu_custom_call" | custom-call | tf_op jit(solution)/shard_map/pallas_call | solution.py:116
  36.7 0.0 collective-permute-done.6.refs_3_
  36.8 16.4 %shard_map.51 = (f32[512,2048]{1,0:T(8,128)}, f32[1,2048]{1,0:T(1,128)S(1)}) custom-call(f32[3,4096]{1,0:T(4,128)S(1)} %get-tuple-element.6.lines_ref, bf16[3,200,2048]{2,1,0:T(8,128)(2,1)S(1)} %get-tuple-element.7.early_ref, bf16[1024,512]{1,0:T(8,128)(2,1)S(1)} %bitcast.13, bf16[50,2048]{1,0:T(8,128)(2,1)S(1)} %collective-permute-done.3.refs_0_, ...), custom_call_target="tpu_custom_call" | custom-call | tf_op jit(solution)/shard_map/pallas_call | solution.py:145
  53.2 7.6 %all_to_all.20 = f32[8,1,2048]{2,1,0:T(1,128)S(1)} all-to-all(f32[8,1,2048]{2,1,0:T(1,128)S(1)} %broadcast_in_dim.42), channel_id=1, replica_groups=mesh['split'=16,'shard'=8] {'shard'}, dimensions={0} | all-to-all | bytes 131072 | tf_op jit(solution)/shard_map/all_to_all | solution.py:18
  60.8 0.1 reduce_max.18
  60.9 0.1 broadcast_in_dim.43
  60.9 13.3 %all_to_all.21 = f32[16,1,2048]{2,1,0:T(1,128)S(1)} all-to-all(f32[16,1,2048]{2,1,0:T(1,128)S(1)} %broadcast_in_dim.43), channel_id=1, replica_groups=mesh['split'=16,'shard'=8] {'split'}, dimensions={0} | all-to-all | bytes 262144 | tf_op jit(solution)/shard_map/all_to_all | solution.py:18
  74.2 0.7 reduce_max.19
  (11 shorter events, 0.1 us)
Async XLA Ops:
  0.6 23.5 %copy-start = (bf16[1,2,512,400]{2,3,1,0:T(8,128)(2,1)S(1)}, bf16[1,2,512,400]{2,3,1,0:T(8,128)(2,1)}, u32[]{:S(2)}) copy-start(bf16[1,2,512,400]{2,3,1,0:T(8,128)(2,1)} %param.5) | copy-start | bytes 2457604
  0.6 22.2 %collective-permute-start.3 = (bf16[50,2048]{1,0:T(8,128)(2,1)}, bf16[50,2048]{1,0:T(8,128)(2,1)S(1)}, u32[]{:S(2)}, u32[]{:S(2)}) collective-permute-start(bf16[50,2048]{1,0:T(8,128)(2,1)} %bitcast.15), channel_id=1, source_target_pairs={{0,2},{1,3},{2,0},{3,1},{4,6},{5,7},{6,4},{7,5},{8,10},{9,11},{10,... | collective-permute-start | bytes 614408 | tf_op jit(solution)/shard_map/ppermute | solution.py:177
  5.2 24.1 %collective-permute-start.2 = (bf16[50,2048]{1,0:T(8,128)(2,1)}, bf16[50,2048]{1,0:T(8,128)(2,1)S(1)}, u32[]{:S(2)}, u32[]{:S(2)}) collective-permute-start(bf16[50,2048]{1,0:T(8,128)(2,1)} %bitcast.16), channel_id=1, source_target_pairs={{0,3},{1,2},{2,1},{3,0},{4,7},{5,6},{6,5},{7,4},{8,11},{9,10},{10,... | collective-permute-start | bytes 614408 | tf_op jit(solution)/shard_map/ppermute | solution.py:177
  5.6 23.7 %collective-permute-start.1 = (bf16[50,2048]{1,0:T(8,128)(2,1)}, bf16[50,2048]{1,0:T(8,128)(2,1)S(1)}, u32[]{:S(2)}, u32[]{:S(2)}) collective-permute-start(bf16[50,2048]{1,0:T(8,128)(2,1)} %bitcast.17), channel_id=1, source_target_pairs={{0,1},{1,0},{2,3},{3,2},{4,5},{5,4},{6,7},{7,6},{8,9},{9,8},{10,11... | collective-permute-start | bytes 614408 | tf_op jit(solution)/shard_map/ppermute | solution.py:177
  5.9 13.6 %collective-permute-start = (bf16[50,2048]{1,0:T(8,128)(2,1)}, bf16[50,2048]{1,0:T(8,128)(2,1)S(1)}, u32[]{:S(2)}, u32[]{:S(2)}) collective-permute-start(bf16[50,2048]{1,0:T(8,128)(2,1)} %bitcast.18), channel_id=1, source_target_pairs={{0,4},{1,5},{2,6},{3,7},{4,0},{5,1},{6,2},{7,3},{8,12},{9,13},{10,... | collective-permute-start | bytes 614408 | tf_op jit(solution)/shard_map/ppermute | solution.py:177
  8.6 20.7 %all-to-all-start = ((f32[128,1,96]{2,1,0:T(1,128)}), f32[128,1,96]{2,1,0:T(1,128)S(1)}, u32[]{:S(2)}, u32[]{:S(2)}) async-start(f32[128,1,96]{2,1,0:T(1,128)} %broadcast_in_dim.38), calls=%async_computation | async-start | bytes 131072 | tf_op jit(solution)/shard_map/all_to_all | solution.py:18
  19.5 17.2 %collective-permute-start.5 = (bf16[50,2048]{1,0:T(8,128)(2,1)S(1)}, bf16[50,2048]{1,0:T(8,128)(2,1)S(1)}, u32[]{:S(2)}, u32[]{:S(2)}) collective-permute-start(bf16[50,2048]{1,0:T(8,128)(2,1)S(1)} %collective-permute-done.refs_1_), channel_id=1, source_target_pairs={{0,3},{1,2},{2,1},{3,0},{4,7},{5,6},{6,5},{7,4},{8,11},{9,10},{10,... | collective-permute-start | bytes 614408 | tf_op jit(solution)/shard_map/ppermute | solution.py:177
  22.9 13.9 %collective-permute-start.4 = (bf16[50,2048]{1,0:T(8,128)(2,1)S(1)}, bf16[50,2048]{1,0:T(8,128)(2,1)S(1)}, u32[]{:S(2)}, u32[]{:S(2)}) collective-permute-start(bf16[50,2048]{1,0:T(8,128)(2,1)S(1)} %collective-permute-done.refs_1_), channel_id=1, source_target_pairs={{0,1},{1,0},{2,3},{3,2},{4,5},{5,4},{6,7},{7,6},{8,9},{9,8},{10,11... | collective-permute-start | bytes 614408 | tf_op jit(solution)/shard_map/ppermute | solution.py:177
  22.9 13.9 %collective-permute-start.6 = (bf16[50,2048]{1,0:T(8,128)(2,1)S(1)}, bf16[50,2048]{1,0:T(8,128)(2,1)}, u32[]{:S(2)}, u32[]{:S(2)}) collective-permute-start(bf16[50,2048]{1,0:T(8,128)(2,1)S(1)} %collective-permute-done.3.refs_0_), channel_id=1, source_target_pairs={{0,4},{1,5},{2,6},{3,7},{4,0},{5,1},{6,2},{7,3},{8,12},{9,13},{10,... | collective-permute-start | bytes 614408 | tf_op jit(solution)/shard_map/ppermute | solution.py:177
  24.1 5.1 %copy-start.1 = (bf16[1,50,2048]{2,1,0:T(8,128)(2,1)S(1)}, bf16[1,50,2048]{2,1,0:T(8,128)(2,1)}, u32[]{:S(2)}) copy-start(bf16[1,50,2048]{2,1,0:T(8,128)(2,1)} %param.4) | copy-start | bytes 614404

commit v3 on v2

--- a/solution.py
+++ b/solution.py
@@ -10,7 +10,7 @@
 VMEM = pltpu.VMEM
 LIMIT = 30 << 20
 COLS = 512
-EARLY = 4
+EARLY = 3
 
 
 def spread(block, axes, count):
@@ -44,9 +44,7 @@
             slab_ref[det, row : row + 16, :] = pair[:, 128 * q : 128 * q + cols]
 
 
-def prepare(lines_ref, block_refs, slab_ref, basis_ref):
-    for det in range(slab_ref.shape[0]):
-        fill_slab(lines_ref[det : det + 1, :], slab_ref, det)
+def stack_blocks(block_refs, basis_ref):
     row = 0
     for block_ref in block_refs:
         each = block_ref.shape[0]
@@ -63,28 +61,30 @@
 
 def early_kernel(parts_ref, *refs, blocks):
     block_refs = refs[:blocks]
-    out_ref, lines_ref, basis_ref, slab_ref, turned_ref = refs[blocks:]
+    out_ref, slab_ref, lines_ref, basis_ref, turned_ref = refs[blocks:]
     step = pl.program_id(0)
 
     @pl.when(step == 0)
     def _():
         join_strain(parts_ref, lines_ref, turned_ref)
-        prepare(lines_ref, block_refs, slab_ref, basis_ref)
+        for det in range(slab_ref.shape[0]):
+            fill_slab(lines_ref[det : det + 1, :], slab_ref, det)
+        stack_blocks(block_refs, basis_ref)
 
     for det in range(out_ref.shape[0]):
         out_ref[det] = filtered(basis_ref, slab_ref, det, step, pl.num_programs(0))
 
 
-def late_kernel(lines_ref, early_ref, weights_ref, *refs, blocks):
+def late_kernel(slab_ref, early_ref, weights_ref, *refs, blocks):
     block_refs = refs[:blocks]
-    snr_ref, peak_ref, basis_ref, slab_ref, series_ref = refs[blocks:]
+    snr_ref, peak_ref, basis_ref, series_ref = refs[blocks:]
     step, steps = pl.program_id(0), pl.num_programs(0)
     ndet, nearly = early_ref.shape[:2]
     nlate = basis_ref.shape[0]
 
     @pl.when(step == 0)
     def _():
-        prepare(lines_ref, block_refs, slab_ref, basis_ref)
+        stack_blocks(block_refs, basis_ref)
         series_ref[...] = jnp.zeros_like(series_ref)
 
     templ = weights_ref.shape[0] // 2
@@ -119,25 +119,24 @@
         in_specs=[pl.BlockSpec(memory_space=VMEM)] * (len(blocks) + 1),
         out_specs=[
             pl.BlockSpec((ndet, nearly, COLS), lambda i: (0, 0, i)),
-            pl.BlockSpec((ndet, samples), lambda i: (0, 0)),
+            pl.BlockSpec(memory_space=VMEM),
         ],
         out_shape=[
             jax.ShapeDtypeStruct((ndet, nearly, tout), jnp.bfloat16),
-            jax.ShapeDtypeStruct((ndet, samples), jnp.float32),
+            jax.ShapeDtypeStruct((ndet, samples - COLS, COLS), jnp.bfloat16),
         ],
         scratch_shapes=[
+            VMEM((ndet, samples), jnp.float32),
             VMEM((nearly, taps), jnp.bfloat16),
-            VMEM((ndet, samples - COLS, COLS), jnp.bfloat16),
             VMEM((samples // 128, 128), jnp.float32),
         ],
         compiler_params=pltpu.CompilerParams(vmem_limit_bytes=LIMIT),
     )(parts, *blocks)
 
 
-def bank(lines, early, blocks, weights):
+def bank(slab, early, blocks, weights):
     ndet, nearly, tout = early.shape
     taps = blocks[0].shape[1]
-    samples = tout + taps
     nlate = sum(block.shape[0] for block in blocks)
     templ, depth = weights.shape[0] // 2, weights.shape[1]
     steps = tout // COLS
@@ -157,11 +156,10 @@
         ],
         scratch_shapes=[
             VMEM((nlate, taps), jnp.bfloat16),
-            VMEM((ndet, samples - COLS, COLS), jnp.bfloat16),
             VMEM((ndet, depth, COLS), jnp.bfloat16),
         ],
         compiler_params=pltpu.CompilerParams(vmem_limit_bytes=LIMIT),
-    )(lines, early, weights, *blocks)
+    )(slab, early, weights, *blocks)
 
 
 def per_device(strain, basis, recon, nsplit, nshard):
@@ -176,13 +174,12 @@
         pairs = [(i, i ^ away) for i in range(nshard)]
         return lax.ppermute(block, "shard", pairs)
 
-    got = {0: own}
-    for away in (4, 1, 3, 2):
-        got[away] = swap(own, away)
-    got[5] = swap(got[4], 1)
-    got[7] = swap(got[4], 3)
+    got = {0: own, 4: swap(own, 4), 2: swap(own, 2)}
     got[6] = swap(got[2], 4)
-    far = [0, 4, 1, 3, 2, 5, 7, 6]
+    later, _ = lax.optimization_barrier((own, got[4]))
+    got[1], got[3] = swap(later, 1), swap(later, 3)
+    got[5], got[7] = swap(got[4], 1), swap(got[4], 3)
+    far = [0, 4, 2, 6, 1, 3, 5, 7]
     blocks = [got[away] for away in far]
 
     nbasis = each * nshard
@@ -197,8 +194,8 @@
     weights = jnp.einsum("qml,lp->qmp", recon[0], order, preferred_element_type=jnp.float32)
     weights = weights.astype(jnp.bfloat16).reshape(-1, depth)
 
-    early, lines = early_series(parts, blocks[:EARLY], strain.shape[0])
-    snr, peak = bank(lines, early, blocks[EARLY:], weights)
+    early, slab = early_series(parts, blocks[:EARLY], strain.shape[0])
+    snr, peak = bank(slab, early, blocks[EARLY:], weights)
 
     peak = jnp.max(spread(peak.reshape(-1), "shard", nshard), axis=0)
     loudest = jnp.max(spread(peak, "split", nsplit), axis=0)

time: 75.2 us -> 72.9 us (0.969)
  blocking collectives: 20.8 us -> 23.5 us
  starting transfers between devices: 22 us -> 19.8 us
  waiting for transfers between devices: 4.32 us -> 2.85 us
  Pallas kernels: 23.9 us -> 22.6 us
    all_to_all x1, starting transfers between devices: 10.9 us -> 7.91 us  [spread(): return lax.all_to_all(copies, axes, 0, 0, tiled=True)]
    all_to_all x2, blocking collectives: 20.8 us -> 23.5 us  [spread(): return lax.all_to_all(copies, axes, 0, 0, tiled=True)]
    all_to_all x1, waiting for transfers between devices: 4.3 us -> 2.83 us  [spread(): return lax.all_to_all(copies, axes, 0, 0, tiled=True)]
    pallas_call x1, Pallas kernels: 16.4 us -> 15.5 us  [bank(): pl.pallas_call(functools.partial(late_kernel, blocks=len(blocks)), grid=(...]
where the time goes in v3:
time: 72.9 us; the launch traced here: 72.6 us
  blocking collectives  23.5 us (32%)
  Pallas kernels  22.6 us (31%)
  starting transfers between devices  19.8 us (27%)
  waiting for transfers between devices  2.85 us (4%)
  local copies, waits for them, and re-layouts  1.55 us (2%)
  matrix products  0.82 us (1%)
  other arithmetic  0.78 us (1%)
  between operations  0.76 us (1%)
    all_to_all x2, blocking collectives, spread(): return lax.all_to_all(copies, axes, 0, 0, tiled=True)  23.5 us
    pallas_call x1, Pallas kernels, bank(): pl.pallas_call(functools.partial(late_kernel, blocks=len(blocks)), grid=(...  15.5 us
    ppermute x7, starting transfers between devices, swap(): return lax.ppermute(block, 'shard', pairs)  11.9 us
    all_to_all x1, starting transfers between devices, spread(): return lax.all_to_all(copies, axes, 0, 0, tiled=True)  7.91 us
    pallas_call x1, Pallas kernels, early_series(): pl.pallas_call(functools.partial(early_kernel, blocks=len(blocks)), grid=...  7.08 us
    all_to_all x1, waiting for transfers between devices, spread(): return lax.all_to_all(copies, axes, 0, 0, tiled=True)  2.83 us
    broadcast_in_dim x4, local copies, waits for them, and re-layouts, spread(): copies = jnp.broadcast_to(block[None], (count,) + block.shape)  1.53 us
  transfers between devices with their start and end apart: 8, of which 1 were waited for; matrix products, arithmetic and copies ran while one was open for 3% of the time, Pallas kernels for 10%

profile of v3, /device:TPU:1, one launch (start us, length us, event | category | flops | bytes accessed | tf_op | source)
XLA Modules:
  0.0 72.6 jit_solution(13399012318929301150)
XLA Ops:
  0.6 0.0 copy-start
  0.6 0.0 copy-start.1
  0.7 4.5 %collective-permute-start.1 = (bf16[50,2048]{1,0:T(8,128)(2,1)}, bf16[50,2048]{1,0:T(8,128)(2,1)}, u32[]{:S(2)}, u32[]{:S(2)}) collective-permute-start(bf16[50,2048]{1,0:T(8,128)(2,1)} %bitcast.15), channel_id=1, source_target_pairs={{0,2},{1,3},{2,0},{3,1},{4,6},{5,7},{6,4},{7,5},{8,10},{9,11},{10,... | collective-permute-start | bytes 614408 | tf_op jit(solution)/shard_map/ppermute | solution.py:175
  5.2 1.3 %collective-permute-start = (bf16[50,2048]{1,0:T(8,128)(2,1)}, bf16[50,2048]{1,0:T(8,128)(2,1)S(1)}, u32[]{:S(2)}, u32[]{:S(2)}) collective-permute-start(bf16[50,2048]{1,0:T(8,128)(2,1)} %bitcast.16), channel_id=1, source_target_pairs={{0,4},{1,5},{2,6},{3,7},{4,0},{5,1},{6,2},{7,3},{8,12},{9,13},{10,... | collective-permute-start | bytes 614408 | tf_op jit(solution)/shard_map/ppermute | solution.py:175
  6.5 0.8 %reshape.29 = f32[96]{0:T(128)S(1)} reshape(bf16[3,32]{1,0:T(4,128)(2,1)} %param.3) | data formatting | bytes 576 | tf_op jit(solution)/shard_map/broadcast_in_dim | solution.py:17
  7.2 0.7 broadcast_in_dim.38
  7.9 7.9 %all-to-all-start = ((f32[128,1,96]{2,1,0:T(1,128)}), f32[128,1,96]{2,1,0:T(1,128)S(1)}, u32[]{:S(2)}, u32[]{:S(2)}) async-start(f32[128,1,96]{2,1,0:T(1,128)} %broadcast_in_dim.38), calls=%async_computation | async-start | bytes 131072 | tf_op jit(solution)/shard_map/all_to_all | solution.py:18
  15.9 0.0 collective-permute-done.refs_1_
  15.9 3.3 %collective-permute-start.4 = (bf16[50,2048]{1,0:T(8,128)(2,1)}, bf16[50,2048]{1,0:T(8,128)(2,1)S(1)}, u32[]{:S(2)}, u32[]{:S(2)}) collective-permute-start(bf16[50,2048]{1,0:T(8,128)(2,1)} %bitcast.17), channel_id=1, source_target_pairs={{0,3},{1,2},{2,1},{3,0},{4,7},{5,6},{6,5},{7,4},{8,11},{9,10},{10,... | collective-permute-start | bytes 614408 | tf_op jit(solution)/shard_map/ppermute | solution.py:175
  19.2 0.4 collective-permute-start.6
  19.6 1.1 %collective-permute-start.5 = (bf16[50,2048]{1,0:T(8,128)(2,1)S(1)}, bf16[50,2048]{1,0:T(8,128)(2,1)S(1)}, u32[]{:S(2)}, u32[]{:S(2)}) collective-permute-start(bf16[50,2048]{1,0:T(8,128)(2,1)S(1)} %collective-permute-done.refs_1_), channel_id=1, source_target_pairs={{0,1},{1,0},{2,3},{3,2},{4,5},{5,4},{6,7},{7,6},{8,9},{9,8},{10,11... | collective-permute-start | bytes 614408 | tf_op jit(solution)/shard_map/ppermute | solution.py:175
  20.7 1.3 %collective-permute-start.2 = (bf16[50,2048]{1,0:T(8,128)(2,1)}, bf16[50,2048]{1,0:T(8,128)(2,1)S(1)}, u32[]{:S(2)}, u32[]{:S(2)}) collective-permute-start(bf16[50,2048]{1,0:T(8,128)(2,1)} %collective-permute-done.1.refs_2_), channel_id=1, source_target_pairs={{0,4},{1,5},{2,6},{3,7},{4,0},{5,1},{6,2},{7,3},{8,12},{9,13},{10,... | collective-permute-start | bytes 614408 | tf_op jit(solution)/shard_map/ppermute | solution.py:175
  21.9 0.8 %convolution_convert_fusion = bf16[512,2,512]{0,2,1:T(8,128)(2,1)S(1)} fusion(bf16[1,2,512,400]{2,3,1,0:T(8,128)(2,1)S(1)} %copy-done, s32[512]{0:T(512)S(1)} %get-tuple-element.13, s32[512]{0:T(512)S(1)} %get-tuple-element.14, s32[]{:T(128)S(6)} %axis_index.12, s32[512]{0:T(512)S(1)} %get-tuple-element.12, s32[512]{0:T(512)S(1)} %get-tuple-element.15, ...), kind=kOutput, calls=%fused_computation.7 | convolution fusion | flops 424255488 | bytes 1877508 | tf_op jit(solution)/shard_map/qml,lp->qmp/dot_general | solution.py:194
  22.8 2.8 %all-to-all-done = f32[128,1,96]{2,1,0:T(1,128)S(1)} async-done(((f32[128,1,96]{2,1,0:T(1,128)}), f32[128,1,96]{2,1,0:T(1,128)S(1)}, u32[]{:S(2)}, u32[]{:S(2)}) %all-to-all-start) | async-done | bytes 49184 | tf_op jit(solution)/shard_map/all_to_all | solution.py:18
  25.6 7.1 %shard_map.50 = (bf16[3,150,2048]{2,1,0:T(8,128)(2,1)S(1)}, bf16[3,3584,512]{2,1,0:T(8,128)(2,1)S(1)}) custom-call(f32[128,96]{1,0:T(8,128)S(1)} %bitcast.14, bf16[50,2048]{1,0:T(8,128)(2,1)S(1)} %bitcast.19, bf16[50,2048]{1,0:T(8,128)(2,1)S(1)} %collective-permute-done.refs_1_, bf16[50,2048]{1,0:T(8,128)(2,1)} %collective-permute-done.1.refs_2_), custom_call_target="tpu_custom_call" | custom-call | tf_op jit(solution)/shard_map/pallas_call | solution.py:116
  32.7 0.0 collective-permute-done.4.refs_2_
  32.7 0.0 collective-permute-done.3.refs_1_
  32.7 0.0 collective-permute-done.5.refs_3_
  32.7 15.5 %shard_map.51 = (f32[512,2048]{1,0:T(8,128)}, f32[1,2048]{1,0:T(1,128)S(1)}) custom-call(bf16[3,3584,512]{2,1,0:T(8,128)(2,1)S(1)} %get-tuple-element.7.slab_ref, bf16[3,150,2048]{2,1,0:T(8,128)(2,1)S(1)} %get-tuple-element.8.early_ref, bf16[1024,512]{1,0:T(8,128)(2,1)S(1)} %bitcast.13, bf16[50,2048]{1,0:T(8,128)(2,1)S(1)} %collective-permute-done.2.refs_0_, ...), custom_call_target="tpu_custom_call" | custom-call | tf_op jit(solution)/shard_map/pallas_call | solution.py:144
  48.3 7.6 %all_to_all.20 = f32[8,1,2048]{2,1,0:T(1,128)S(1)} all-to-all(f32[8,1,2048]{2,1,0:T(1,128)S(1)} %broadcast_in_dim.42), channel_id=1, replica_groups=mesh['split'=16,'shard'=8] {'shard'}, dimensions={0} | all-to-all | bytes 131072 | tf_op jit(solution)/shard_map/all_to_all | solution.py:18
  55.9 0.1 reduce_max.18
  55.9 0.1 broadcast_in_dim.43
  56.0 15.9 %all_to_all.21 = f32[16,1,2048]{2,1,0:T(1,128)S(1)} all-to-all(f32[16,1,2048]{2,1,0:T(1,128)S(1)} %broadcast_in_dim.43), channel_id=1, replica_groups=mesh['split'=16,'shard'=8] {'split'}, dimensions={0} | all-to-all | bytes 262144 | tf_op jit(solution)/shard_map/all_to_all | solution.py:18
  71.9 0.7 reduce_max.19
  (11 shorter events, 0.1 us)
Async XLA Ops:
  0.6 21.3 %copy-start = (bf16[1,2,512,400]{2,3,1,0:T(8,128)(2,1)S(1)}, bf16[1,2,512,400]{2,3,1,0:T(8,128)(2,1)}, u32[]{:S(2)}) copy-start(bf16[1,2,512,400]{2,3,1,0:T(8,128)(2,1)} %param.5) | copy-start | bytes 2457604
  0.6 25.0 %copy-start.1 = (bf16[1,50,2048]{2,1,0:T(8,128)(2,1)S(1)}, bf16[1,50,2048]{2,1,0:T(8,128)(2,1)}, u32[]{:S(2)}) copy-start(bf16[1,50,2048]{2,1,0:T(8,128)(2,1)} %param.4) | copy-start | bytes 614404
  0.7 20.0 %collective-permute-start.1 = (bf16[50,2048]{1,0:T(8,128)(2,1)}, bf16[50,2048]{1,0:T(8,128)(2,1)}, u32[]{:S(2)}, u32[]{:S(2)}) collective-permute-start(bf16[50,2048]{1,0:T(8,128)(2,1)} %bitcast.15), channel_id=1, source_target_pairs={{0,2},{1,3},{2,0},{3,1},{4,6},{5,7},{6,4},{7,5},{8,10},{9,11},{10,... | collective-permute-start | bytes 614408 | tf_op jit(solution)/shard_map/ppermute | solution.py:175
  5.2 10.7 %collective-permute-start = (bf16[50,2048]{1,0:T(8,128)(2,1)}, bf16[50,2048]{1,0:T(8,128)(2,1)S(1)}, u32[]{:S(2)}, u32[]{:S(2)}) collective-permute-start(bf16[50,2048]{1,0:T(8,128)(2,1)} %bitcast.16), channel_id=1, source_target_pairs={{0,4},{1,5},{2,6},{3,7},{4,0},{5,1},{6,2},{7,3},{8,12},{9,13},{10,... | collective-permute-start | bytes 614408 | tf_op jit(solution)/shard_map/ppermute | solution.py:175
  7.9 17.7 %all-to-all-start = ((f32[128,1,96]{2,1,0:T(1,128)}), f32[128,1,96]{2,1,0:T(1,128)S(1)}, u32[]{:S(2)}, u32[]{:S(2)}) async-start(f32[128,1,96]{2,1,0:T(1,128)} %broadcast_in_dim.38), calls=%async_computation | async-start | bytes 131072 | tf_op jit(solution)/shard_map/all_to_all | solution.py:18
  15.9 16.8 %collective-permute-start.4 = (bf16[50,2048]{1,0:T(8,128)(2,1)}, bf16[50,2048]{1,0:T(8,128)(2,1)S(1)}, u32[]{:S(2)}, u32[]{:S(2)}) collective-permute-start(bf16[50,2048]{1,0:T(8,128)(2,1)} %bitcast.17), channel_id=1, source_target_pairs={{0,3},{1,2},{2,1},{3,0},{4,7},{5,6},{6,5},{7,4},{8,11},{9,10},{10,... | collective-permute-start | bytes 614408 | tf_op jit(solution)/shard_map/ppermute | solution.py:175
  19.2 13.5 %collective-permute-start.3 = (bf16[50,2048]{1,0:T(8,128)(2,1)}, bf16[50,2048]{1,0:T(8,128)(2,1)S(1)}, u32[]{:S(2)}, u32[]{:S(2)}) collective-permute-start(bf16[50,2048]{1,0:T(8,128)(2,1)} %bitcast.18), channel_id=1, source_target_pairs={{0,1},{1,0},{2,3},{3,2},{4,5},{5,4},{6,7},{7,6},{8,9},{9,8},{10,11... | collective-permute-start | bytes 614408 | tf_op jit(solution)/shard_map/ppermute | solution.py:175
  19.2 13.5 %collective-permute-start.6 = (bf16[50,2048]{1,0:T(8,128)(2,1)S(1)}, bf16[50,2048]{1,0:T(8,128)(2,1)S(1)}, u32[]{:S(2)}, u32[]{:S(2)}) collective-permute-start(bf16[50,2048]{1,0:T(8,128)(2,1)S(1)} %collective-permute-done.refs_1_), channel_id=1, source_target_pairs={{0,3},{1,2},{2,1},{3,0},{4,7},{5,6},{6,5},{7,4},{8,11},{9,10},{10,... | collective-permute-start | bytes 614408 | tf_op jit(solution)/shard_map/ppermute | solution.py:175
  19.6 13.1 %collective-permute-start.5 = (bf16[50,2048]{1,0:T(8,128)(2,1)S(1)}, bf16[50,2048]{1,0:T(8,128)(2,1)S(1)}, u32[]{:S(2)}, u32[]{:S(2)}) collective-permute-start(bf16[50,2048]{1,0:T(8,128)(2,1)S(1)} %collective-permute-done.refs_1_), channel_id=1, source_target_pairs={{0,1},{1,0},{2,3},{3,2},{4,5},{5,4},{6,7},{7,6},{8,9},{9,8},{10,11... | collective-permute-start | bytes 614408 | tf_op jit(solution)/shard_map/ppermute | solution.py:175
  20.7 12.0 %collective-permute-start.2 = (bf16[50,2048]{1,0:T(8,128)(2,1)}, bf16[50,2048]{1,0:T(8,128)(2,1)S(1)}, u32[]{:S(2)}, u32[]{:S(2)}) collective-permute-start(bf16[50,2048]{1,0:T(8,128)(2,1)} %collective-permute-done.1.refs_2_), channel_id=1, source_target_pairs={{0,4},{1,5},{2,6},{3,7},{4,0},{5,1},{6,2},{7,3},{8,12},{9,13},{10,... | collective-permute-start | bytes 614408 | tf_op jit(solution)/shard_map/ppermute | solution.py:175

commit v4 on v3

--- a/solution.py
+++ b/solution.py
@@ -85,7 +85,6 @@
     @pl.when(step == 0)
     def _():
         stack_blocks(block_refs, basis_ref)
-        series_ref[...] = jnp.zeros_like(series_ref)
 
     templ = weights_ref.shape[0] // 2
 
@@ -94,15 +93,16 @@
         late = filtered(basis_ref, slab_ref, det, step, steps)
         series_ref[det, nearly : nearly + nlate, :] = late
 
+    nbasis = nearly + nlate
     total = None
     fill(0)
     for det in range(ndet):
         if det + 1 < ndet:
             fill(det + 1)
-        zvals = jnp.dot(weights_ref[...], series_ref[det], preferred_element_type=jnp.float32)
-        power = zvals * zvals
-        both = power[:templ] + power[templ:]
-        total = both if total is None else total + both
+        for quad in range(2):
+            rows = weights_ref[quad * templ : (quad + 1) * templ, :nbasis]
+            zvals = jnp.dot(rows, series_ref[det], preferred_element_type=jnp.float32)
+            total = zvals * zvals if total is None else total + zvals * zvals
     snr = total * (1.0 / (2.0 * ndet))
     snr_ref[...] = snr
     peak_ref[...] = jnp.max(snr, axis=0, keepdims=True)
@@ -138,7 +138,7 @@
     ndet, nearly, tout = early.shape
     taps = blocks[0].shape[1]
     nlate = sum(block.shape[0] for block in blocks)
-    templ, depth = weights.shape[0] // 2, weights.shape[1]
+    templ = weights.shape[0] // 2
     steps = tout // COLS
     whole = pl.BlockSpec(memory_space=VMEM)
     return pl.pallas_call(
@@ -156,10 +156,29 @@
         ],
         scratch_shapes=[
             VMEM((nlate, taps), jnp.bfloat16),
-            VMEM((ndet, depth, COLS), jnp.bfloat16),
+            VMEM((ndet, nearly + nlate, COLS), jnp.bfloat16),
         ],
         compiler_params=pltpu.CompilerParams(vmem_limit_bytes=LIMIT),
     )(slab, early, weights, *blocks)
+
+
+def copy_kernel(strain_ref, copies_ref):
+    ndet, piece = strain_ref.shape
+    for det in range(ndet):
+        row = strain_ref[det : det + 1, :].astype(jnp.float32)
+        copies_ref[:, det * piece : (det + 1) * piece] = jnp.broadcast_to(
+            row, (copies_ref.shape[0], piece)
+        )
+
+
+def strain_copies(strain, count):
+    return pl.pallas_call(
+        copy_kernel,
+        in_specs=[pl.BlockSpec(memory_space=VMEM)],
+        out_specs=pl.BlockSpec(memory_space=VMEM),
+        out_shape=jax.ShapeDtypeStruct((count, strain.size), jnp.float32),
+        compiler_params=pltpu.CompilerParams(vmem_limit_bytes=LIMIT),
+    )(strain)
 
 
 def per_device(strain, basis, recon, nsplit, nshard):
@@ -168,7 +187,8 @@
     count = nsplit * nshard
     me = lax.axis_index("shard")
 
-    parts = spread(strain.astype(jnp.float32).reshape(-1), ("split", "shard"), count)
+    copies = strain_copies(strain, count)
+    parts = lax.all_to_all(copies, ("split", "shard"), 0, 0, tiled=True)
 
     def swap(block, away):
         pairs = [(i, i ^ away) for i in range(nshard)]

time: 72.9 us -> 72.4 us (level)
  local copies, waits for them, and re-layouts: 1.55 us -> 0.8 us
    broadcast_in_dim x4 -> x2, local copies, waits for them, and re-layouts: 1.53 us -> 0.1 us  [spread(): copies = jnp.broadcast_to(block[None], (count,) + block.shape)]
  transfers between devices with their start and end apart: 8 -> 8, of which waited for: 1 -> 1; matrix products, arithmetic and copies ran while one was open for 3% -> 1% of each run, Pallas kernels for 10% -> 11%
where the time goes in v4:
time: 72.4 us; the launch traced here: 72.1 us
  blocking collectives  23.5 us (32%)
  Pallas kernels  22.9 us (32%)
  starting transfers between devices  19.8 us (27%)
  waiting for transfers between devices  2.85 us (4%)
  matrix products  0.82 us (1%)
  local copies, waits for them, and re-layouts  0.8 us (1%)
  other arithmetic  0.78 us (1%)
  between operations  0.76 us (1%)
    all_to_all x2, blocking collectives, spread(): return lax.all_to_all(copies, axes, 0, 0, tiled=True)  23.5 us
    pallas_call x1, Pallas kernels, bank(): pl.pallas_call(functools.partial(late_kernel, blocks=len(blocks)), grid=(...  15.1 us
    ppermute x7, starting transfers between devices, swap(): return lax.ppermute(block, 'shard', pairs)  11.9 us
    all_to_all x1, starting transfers between devices, per_device(): parts = lax.all_to_all(copies, ('split', 'shard'), 0, 0, tiled=True)  7.91 us
    pallas_call x1, Pallas kernels, early_series(): pl.pallas_call(functools.partial(early_kernel, blocks=len(blocks)), grid=...  7.08 us
    all_to_all x1, waiting for transfers between devices, per_device(): parts = lax.all_to_all(copies, ('split', 'shard'), 0, 0, tiled=True)  2.83 us
  transfers between devices with their start and end apart: 8, of which 1 were waited for; matrix products, arithmetic and copies ran while one was open for 1% of the time, Pallas kernels for 11%

profile of v4, /device:TPU:1, one launch (start us, length us, event | category | flops | bytes accessed | tf_op | source)
XLA Modules:
  0.0 72.1 jit_solution(17183391972077289928)
XLA Ops:
  0.6 0.0 copy-start
  0.6 0.0 copy-start.1
  0.7 4.5 %collective-permute-start.1 = (bf16[50,2048]{1,0:T(8,128)(2,1)}, bf16[50,2048]{1,0:T(8,128)(2,1)}, u32[]{:S(2)}, u32[]{:S(2)}) collective-permute-start(bf16[50,2048]{1,0:T(8,128)(2,1)} %bitcast.18), channel_id=1, source_target_pairs={{0,2},{1,3},{2,0},{3,1},{4,6},{5,7},{6,4},{7,5},{8,10},{9,11},{10,... | collective-permute-start | bytes 614408 | tf_op jit(solution)/shard_map/ppermute | solution.py:195
  5.2 1.3 %collective-permute-start = (bf16[50,2048]{1,0:T(8,128)(2,1)}, bf16[50,2048]{1,0:T(8,128)(2,1)S(1)}, u32[]{:S(2)}, u32[]{:S(2)}) collective-permute-start(bf16[50,2048]{1,0:T(8,128)(2,1)} %bitcast.19), channel_id=1, source_target_pairs={{0,4},{1,5},{2,6},{3,7},{4,0},{5,1},{6,2},{7,3},{8,12},{9,13},{10,... | collective-permute-start | bytes 614408 | tf_op jit(solution)/shard_map/ppermute | solution.py:195
  6.5 0.7 copy-done.2
  7.1 0.7 shard_map.50
  7.8 7.9 %all-to-all-start = ((f32[128,1,96]{2,1,0:T(1,128)}), f32[128,1,96]{2,1,0:T(1,128)S(1)}, u32[]{:S(2)}, u32[]{:S(2)}) async-start(f32[128,1,96]{2,1,0:T(1,128)} %bitcast.1), calls=%async_computation | async-start | bytes 131072 | tf_op jit(solution)/shard_map/all_to_all | solution.py:191
  15.8 0.0 collective-permute-done.refs_1_
  15.8 3.3 %collective-permute-start.4 = (bf16[50,2048]{1,0:T(8,128)(2,1)}, bf16[50,2048]{1,0:T(8,128)(2,1)S(1)}, u32[]{:S(2)}, u32[]{:S(2)}) collective-permute-start(bf16[50,2048]{1,0:T(8,128)(2,1)} %bitcast.20), channel_id=1, source_target_pairs={{0,3},{1,2},{2,1},{3,0},{4,7},{5,6},{6,5},{7,4},{8,11},{9,10},{10,... | collective-permute-start | bytes 614408 | tf_op jit(solution)/shard_map/ppermute | solution.py:195
  19.2 0.0 collective-permute-start.3
  19.2 0.4 collective-permute-start.6
  19.6 1.1 %collective-permute-start.5 = (bf16[50,2048]{1,0:T(8,128)(2,1)S(1)}, bf16[50,2048]{1,0:T(8,128)(2,1)S(1)}, u32[]{:S(2)}, u32[]{:S(2)}) collective-permute-start(bf16[50,2048]{1,0:T(8,128)(2,1)S(1)} %collective-permute-done.refs_1_), channel_id=1, source_target_pairs={{0,1},{1,0},{2,3},{3,2},{4,5},{5,4},{6,7},{7,6},{8,9},{9,8},{10,11... | collective-permute-start | bytes 614408 | tf_op jit(solution)/shard_map/ppermute | solution.py:195
  20.6 1.3 %collective-permute-start.2 = (bf16[50,2048]{1,0:T(8,128)(2,1)}, bf16[50,2048]{1,0:T(8,128)(2,1)S(1)}, u32[]{:S(2)}, u32[]{:S(2)}) collective-permute-start(bf16[50,2048]{1,0:T(8,128)(2,1)} %collective-permute-done.1.refs_2_), channel_id=1, source_target_pairs={{0,4},{1,5},{2,6},{3,7},{4,0},{5,1},{6,2},{7,3},{8,12},{9,13},{10,... | collective-permute-start | bytes 614408 | tf_op jit(solution)/shard_map/ppermute | solution.py:195
  21.9 0.8 %convolution_convert_fusion = bf16[512,2,512]{0,2,1:T(8,128)(2,1)S(1)} fusion(bf16[1,2,512,400]{2,3,1,0:T(8,128)(2,1)S(1)} %copy-done, s32[512]{0:T(512)S(1)} %get-tuple-element.13, s32[512]{0:T(512)S(1)} %get-tuple-element.14, s32[]{:T(128)S(6)} %axis_index.12, s32[512]{0:T(512)S(1)} %get-tuple-element.12, s32[512]{0:T(512)S(1)} %get-tuple-element.15, ...), kind=kOutput, calls=%fused_computation.7 | convolution fusion | flops 424255488 | bytes 1877508 | tf_op jit(solution)/shard_map/qml,lp->qmp/dot_general | solution.py:214
  22.7 2.8 %all-to-all-done = f32[128,1,96]{2,1,0:T(1,128)S(1)} async-done(((f32[128,1,96]{2,1,0:T(1,128)}), f32[128,1,96]{2,1,0:T(1,128)S(1)}, u32[]{:S(2)}, u32[]{:S(2)}) %all-to-all-start) | async-done | bytes 49184 | tf_op jit(solution)/shard_map/all_to_all | solution.py:191
  25.6 7.1 %shard_map.51 = (bf16[3,150,2048]{2,1,0:T(8,128)(2,1)S(1)}, bf16[3,3584,512]{2,1,0:T(8,128)(2,1)S(1)}) custom-call(f32[128,96]{1,0:T(8,128)S(1)} %bitcast.17, bf16[50,2048]{1,0:T(8,128)(2,1)S(1)} %bitcast.22, bf16[50,2048]{1,0:T(8,128)(2,1)S(1)} %collective-permute-done.refs_1_, bf16[50,2048]{1,0:T(8,128)(2,1)} %collective-permute-done.1.refs_2_), custom_call_target="tpu_custom_call" | custom-call | tf_op jit(solution)/shard_map/pallas_call | solution.py:116
  32.6 0.0 collective-permute-done.2.refs_0_
  32.7 0.0 collective-permute-done.6.refs_4_
  32.7 15.1 %shard_map.52 = (f32[512,2048]{1,0:T(8,128)}, f32[1,2048]{1,0:T(1,128)S(1)}) custom-call(bf16[3,3584,512]{2,1,0:T(8,128)(2,1)S(1)} %get-tuple-element.7.slab_ref, bf16[3,150,2048]{2,1,0:T(8,128)(2,1)S(1)} %get-tuple-element.8.early_ref, bf16[1024,512]{1,0:T(8,128)(2,1)S(1)} %bitcast.16, bf16[50,2048]{1,0:T(8,128)(2,1)S(1)} %collective-permute-done.2.refs_0_, ...), custom_call_target="tpu_custom_call" | custom-call | tf_op jit(solution)/shard_map/pallas_call | solution.py:144
  47.8 7.6 %all_to_all.23 = f32[8,1,2048]{2,1,0:T(1,128)S(1)} all-to-all(f32[8,1,2048]{2,1,0:T(1,128)S(1)} %broadcast_in_dim.30), channel_id=1, replica_groups=mesh['split'=16,'shard'=8] {'shard'}, dimensions={0} | all-to-all | bytes 131072 | tf_op jit(solution)/shard_map/all_to_all | solution.py:18
  55.4 0.1 reduce_max.18
  55.5 0.1 broadcast_in_dim.31
  55.5 15.9 %all_to_all.24 = f32[16,1,2048]{2,1,0:T(1,128)S(1)} all-to-all(f32[16,1,2048]{2,1,0:T(1,128)S(1)} %broadcast_in_dim.31), channel_id=1, replica_groups=mesh['split'=16,'shard'=8] {'split'}, dimensions={0} | all-to-all | bytes 262144 | tf_op jit(solution)/shard_map/all_to_all | solution.py:18
  71.5 0.7 reduce_max.19
  (12 shorter events, 0.1 us)
Async XLA Ops:
  0.6 21.3 %copy-start = (bf16[1,2,512,400]{2,3,1,0:T(8,128)(2,1)S(1)}, bf16[1,2,512,400]{2,3,1,0:T(8,128)(2,1)}, u32[]{:S(2)}) copy-start(bf16[1,2,512,400]{2,3,1,0:T(8,128)(2,1)} %param.5) | copy-start | bytes 2457604
  0.6 24.9 %copy-start.1 = (bf16[1,50,2048]{2,1,0:T(8,128)(2,1)S(1)}, bf16[1,50,2048]{2,1,0:T(8,128)(2,1)}, u32[]{:S(2)}) copy-start(bf16[1,50,2048]{2,1,0:T(8,128)(2,1)} %param.4) | copy-start | bytes 614404
  0.7 20.0 %collective-permute-start.1 = (bf16[50,2048]{1,0:T(8,128)(2,1)}, bf16[50,2048]{1,0:T(8,128)(2,1)}, u32[]{:S(2)}, u32[]{:S(2)}) collective-permute-start(bf16[50,2048]{1,0:T(8,128)(2,1)} %bitcast.18), channel_id=1, source_target_pairs={{0,2},{1,3},{2,0},{3,1},{4,6},{5,7},{6,4},{7,5},{8,10},{9,11},{10,... | collective-permute-start | bytes 614408 | tf_op jit(solution)/shard_map/ppermute | solution.py:195
  5.2 10.7 %collective-permute-start = (bf16[50,2048]{1,0:T(8,128)(2,1)}, bf16[50,2048]{1,0:T(8,128)(2,1)S(1)}, u32[]{:S(2)}, u32[]{:S(2)}) collective-permute-start(bf16[50,2048]{1,0:T(8,128)(2,1)} %bitcast.19), channel_id=1, source_target_pairs={{0,4},{1,5},{2,6},{3,7},{4,0},{5,1},{6,2},{7,3},{8,12},{9,13},{10,... | collective-permute-start | bytes 614408 | tf_op jit(solution)/shard_map/ppermute | solution.py:195
  6.5 0.7 copy-start.2
  7.8 17.7 %all-to-all-start = ((f32[128,1,96]{2,1,0:T(1,128)}), f32[128,1,96]{2,1,0:T(1,128)S(1)}, u32[]{:S(2)}, u32[]{:S(2)}) async-start(f32[128,1,96]{2,1,0:T(1,128)} %bitcast.1), calls=%async_computation | async-start | bytes 131072 | tf_op jit(solution)/shard_map/all_to_all | solution.py:191
  15.8 16.8 %collective-permute-start.4 = (bf16[50,2048]{1,0:T(8,128)(2,1)}, bf16[50,2048]{1,0:T(8,128)(2,1)S(1)}, u32[]{:S(2)}, u32[]{:S(2)}) collective-permute-start(bf16[50,2048]{1,0:T(8,128)(2,1)} %bitcast.20), channel_id=1, source_target_pairs={{0,3},{1,2},{2,1},{3,0},{4,7},{5,6},{6,5},{7,4},{8,11},{9,10},{10,... | collective-permute-start | bytes 614408 | tf_op jit(solution)/shard_map/ppermute | solution.py:195
  19.2 13.5 %collective-permute-start.3 = (bf16[50,2048]{1,0:T(8,128)(2,1)}, bf16[50,2048]{1,0:T(8,128)(2,1)S(1)}, u32[]{:S(2)}, u32[]{:S(2)}) collective-permute-start(bf16[50,2048]{1,0:T(8,128)(2,1)} %bitcast.21), channel_id=1, source_target_pairs={{0,1},{1,0},{2,3},{3,2},{4,5},{5,4},{6,7},{7,6},{8,9},{9,8},{10,11... | collective-permute-start | bytes 614408 | tf_op jit(solution)/shard_map/ppermute | solution.py:195
  19.2 13.5 %collective-permute-start.6 = (bf16[50,2048]{1,0:T(8,128)(2,1)S(1)}, bf16[50,2048]{1,0:T(8,128)(2,1)S(1)}, u32[]{:S(2)}, u32[]{:S(2)}) collective-permute-start(bf16[50,2048]{1,0:T(8,128)(2,1)S(1)} %collective-permute-done.refs_1_), channel_id=1, source_target_pairs={{0,3},{1,2},{2,1},{3,0},{4,7},{5,6},{6,5},{7,4},{8,11},{9,10},{10,... | collective-permute-start | bytes 614408 | tf_op jit(solution)/shard_map/ppermute | solution.py:195
  19.6 13.1 %collective-permute-start.5 = (bf16[50,2048]{1,0:T(8,128)(2,1)S(1)}, bf16[50,2048]{1,0:T(8,128)(2,1)S(1)}, u32[]{:S(2)}, u32[]{:S(2)}) collective-permute-start(bf16[50,2048]{1,0:T(8,128)(2,1)S(1)} %collective-permute-done.refs_1_), channel_id=1, source_target_pairs={{0,1},{1,0},{2,3},{3,2},{4,5},{5,4},{6,7},{7,6},{8,9},{9,8},{10,11... | collective-permute-start | bytes 614408 | tf_op jit(solution)/shard_map/ppermute | solution.py:195
  20.6 12.0 %collective-permute-start.2 = (bf16[50,2048]{1,0:T(8,128)(2,1)}, bf16[50,2048]{1,0:T(8,128)(2,1)S(1)}, u32[]{:S(2)}, u32[]{:S(2)}) collective-permute-start(bf16[50,2048]{1,0:T(8,128)(2,1)} %collective-permute-done.1.refs_2_), channel_id=1, source_target_pairs={{0,4},{1,5},{2,6},{3,7},{4,0},{5,1},{6,2},{7,3},{8,12},{9,13},{10,... | collective-permute-start | bytes 614408 | tf_op jit(solution)/shard_map/ppermute | solution.py:195

commit v5 on v4

--- a/solution.py
+++ b/solution.py
@@ -217,8 +217,8 @@
     early, slab = early_series(parts, blocks[:EARLY], strain.shape[0])
     snr, peak = bank(slab, early, blocks[EARLY:], weights)
 
-    peak = jnp.max(spread(peak.reshape(-1), "shard", nshard), axis=0)
-    loudest = jnp.max(spread(peak, "split", nsplit), axis=0)
+    peak = jnp.max(spread(peak.reshape(-1), "split", nsplit), axis=0)
+    loudest = jnp.max(spread(peak, "shard", nshard), axis=0)
     return (snr[None], loudest)
 
 

time: 72.4 us -> 70.8 us (0.978)
  blocking collectives: 23.5 us -> 21.5 us
    all_to_all x2, blocking collectives: 23.5 us -> 21.5 us  [spread(): return lax.all_to_all(copies, axes, 0, 0, tiled=True)]
where the time goes in v5:
time: 70.8 us; the launch traced here: 70.1 us
  Pallas kernels  22.9 us (32%)
  blocking collectives  21.5 us (30%)
  starting transfers between devices  19.8 us (28%)
  waiting for transfers between devices  2.85 us (4%)
  matrix products  0.82 us (1%)
  local copies, waits for them, and re-layouts  0.8 us (1%)
  other arithmetic  0.78 us (1%)
  between operations  0.76 us (1%)
    all_to_all x2, blocking collectives, spread(): return lax.all_to_all(copies, axes, 0, 0, tiled=True)  21.5 us
    pallas_call x1, Pallas kernels, bank(): pl.pallas_call(functools.partial(late_kernel, blocks=len(blocks)), grid=(...  15.1 us
    ppermute x7, starting transfers between devices, swap(): return lax.ppermute(block, 'shard', pairs)  11.9 us
    all_to_all x1, starting transfers between devices, per_device(): parts = lax.all_to_all(copies, ('split', 'shard'), 0, 0, tiled=True)  7.91 us
    pallas_call x1, Pallas kernels, early_series(): pl.pallas_call(functools.partial(early_kernel, blocks=len(blocks)), grid=...  7.08 us
    all_to_all x1, waiting for transfers between devices, per_device(): parts = lax.all_to_all(copies, ('split', 'shard'), 0, 0, tiled=True)  2.83 us
  transfers between devices with their start and end apart: 8, of which 1 were waited for; matrix products, arithmetic and copies ran while one was open for 1% of the time, Pallas kernels for 11%

profile of v5, /device:TPU:1, one launch (start us, length us, event | category | flops | bytes accessed | tf_op | source)
XLA Modules:
  0.0 70.1 jit_solution(1594216926834954855)
XLA Ops:
  0.6 0.0 copy-start
  0.6 0.0 copy-start.1
  0.7 4.5 %collective-permute-start.1 = (bf16[50,2048]{1,0:T(8,128)(2,1)}, bf16[50,2048]{1,0:T(8,128)(2,1)}, u32[]{:S(2)}, u32[]{:S(2)}) collective-permute-start(bf16[50,2048]{1,0:T(8,128)(2,1)} %bitcast.18), channel_id=1, source_target_pairs={{0,2},{1,3},{2,0},{3,1},{4,6},{5,7},{6,4},{7,5},{8,10},{9,11},{10,... | collective-permute-start | bytes 614408 | tf_op jit(solution)/shard_map/ppermute | solution.py:195
  5.2 1.3 %collective-permute-start = (bf16[50,2048]{1,0:T(8,128)(2,1)}, bf16[50,2048]{1,0:T(8,128)(2,1)S(1)}, u32[]{:S(2)}, u32[]{:S(2)}) collective-permute-start(bf16[50,2048]{1,0:T(8,128)(2,1)} %bitcast.19), channel_id=1, source_target_pairs={{0,4},{1,5},{2,6},{3,7},{4,0},{5,1},{6,2},{7,3},{8,12},{9,13},{10,... | collective-permute-start | bytes 614408 | tf_op jit(solution)/shard_map/ppermute | solution.py:195
  6.5 0.7 copy-done.2
  7.1 0.7 %shard_map.50 = f32[128,96]{1,0:T(8,128)} custom-call(bf16[3,32]{1,0:T(4,128)(2,1)S(1)} %copy-done.2), custom_call_target="tpu_custom_call" | custom-call | tf_op jit(solution)/shard_map/pallas_call | solution.py:175
  7.8 7.9 %all-to-all-start = ((f32[128,1,96]{2,1,0:T(1,128)}), f32[128,1,96]{2,1,0:T(1,128)S(1)}, u32[]{:S(2)}, u32[]{:S(2)}) async-start(f32[128,1,96]{2,1,0:T(1,128)} %bitcast.1), calls=%async_computation | async-start | bytes 131072 | tf_op jit(solution)/shard_map/all_to_all | solution.py:191
  15.8 0.0 collective-permute-done.refs_1_
  15.8 3.3 %collective-permute-start.4 = (bf16[50,2048]{1,0:T(8,128)(2,1)}, bf16[50,2048]{1,0:T(8,128)(2,1)S(1)}, u32[]{:S(2)}, u32[]{:S(2)}) collective-permute-start(bf16[50,2048]{1,0:T(8,128)(2,1)} %bitcast.20), channel_id=1, source_target_pairs={{0,3},{1,2},{2,1},{3,0},{4,7},{5,6},{6,5},{7,4},{8,11},{9,10},{10,... | collective-permute-start | bytes 614408 | tf_op jit(solution)/shard_map/ppermute | solution.py:195
  19.2 0.0 collective-permute-start.3
  19.2 0.4 collective-permute-start.6
  19.6 1.1 %collective-permute-start.5 = (bf16[50,2048]{1,0:T(8,128)(2,1)S(1)}, bf16[50,2048]{1,0:T(8,128)(2,1)S(1)}, u32[]{:S(2)}, u32[]{:S(2)}) collective-permute-start(bf16[50,2048]{1,0:T(8,128)(2,1)S(1)} %collective-permute-done.refs_1_), channel_id=1, source_target_pairs={{0,1},{1,0},{2,3},{3,2},{4,5},{5,4},{6,7},{7,6},{8,9},{9,8},{10,11... | collective-permute-start | bytes 614408 | tf_op jit(solution)/shard_map/ppermute | solution.py:195
  20.6 0.0 collective-permute-done.1.refs_2_
  20.6 1.3 %collective-permute-start.2 = (bf16[50,2048]{1,0:T(8,128)(2,1)}, bf16[50,2048]{1,0:T(8,128)(2,1)S(1)}, u32[]{:S(2)}, u32[]{:S(2)}) collective-permute-start(bf16[50,2048]{1,0:T(8,128)(2,1)} %collective-permute-done.1.refs_2_), channel_id=1, source_target_pairs={{0,4},{1,5},{2,6},{3,7},{4,0},{5,1},{6,2},{7,3},{8,12},{9,13},{10,... | collective-permute-start | bytes 614408 | tf_op jit(solution)/shard_map/ppermute | solution.py:195
  21.9 0.8 %convolution_convert_fusion = bf16[512,2,512]{0,2,1:T(8,128)(2,1)S(1)} fusion(bf16[1,2,512,400]{2,3,1,0:T(8,128)(2,1)S(1)} %copy-done, s32[512]{0:T(512)S(1)} %get-tuple-element.13, s32[512]{0:T(512)S(1)} %get-tuple-element.14, s32[]{:T(128)S(6)} %axis_index.12, s32[512]{0:T(512)S(1)} %get-tuple-element.12, s32[512]{0:T(512)S(1)} %get-tuple-element.15, ...), kind=kOutput, calls=%fused_computation.7 | convolution fusion | flops 424255488 | bytes 1877508 | tf_op jit(solution)/shard_map/qml,lp->qmp/dot_general | solution.py:214
  22.7 2.8 %all-to-all-done = f32[128,1,96]{2,1,0:T(1,128)S(1)} async-done(((f32[128,1,96]{2,1,0:T(1,128)}), f32[128,1,96]{2,1,0:T(1,128)S(1)}, u32[]{:S(2)}, u32[]{:S(2)}) %all-to-all-start) | async-done | bytes 49184 | tf_op jit(solution)/shard_map/all_to_all | solution.py:191
  25.6 7.1 %shard_map.51 = (bf16[3,150,2048]{2,1,0:T(8,128)(2,1)S(1)}, bf16[3,3584,512]{2,1,0:T(8,128)(2,1)S(1)}) custom-call(f32[128,96]{1,0:T(8,128)S(1)} %bitcast.17, bf16[50,2048]{1,0:T(8,128)(2,1)S(1)} %bitcast.22, bf16[50,2048]{1,0:T(8,128)(2,1)S(1)} %collective-permute-done.refs_1_, bf16[50,2048]{1,0:T(8,128)(2,1)} %collective-permute-done.1.refs_2_), custom_call_target="tpu_custom_call" | custom-call | tf_op jit(solution)/shard_map/pallas_call | solution.py:116
  32.6 0.0 collective-permute-done.2.refs_0_
  32.7 15.1 %shard_map.52 = (f32[512,2048]{1,0:T(8,128)}, f32[1,2048]{1,0:T(1,128)S(1)}) custom-call(bf16[3,3584,512]{2,1,0:T(8,128)(2,1)S(1)} %get-tuple-element.7.slab_ref, bf16[3,150,2048]{2,1,0:T(8,128)(2,1)S(1)} %get-tuple-element.8.early_ref, bf16[1024,512]{1,0:T(8,128)(2,1)S(1)} %bitcast.16, bf16[50,2048]{1,0:T(8,128)(2,1)S(1)} %collective-permute-done.2.refs_0_, ...), custom_call_target="tpu_custom_call" | custom-call | tf_op jit(solution)/shard_map/pallas_call | solution.py:144
  47.8 0.1 broadcast_in_dim.30
  47.9 13.9 %all_to_all.23 = f32[16,1,2048]{2,1,0:T(1,128)S(1)} all-to-all(f32[16,1,2048]{2,1,0:T(1,128)S(1)} %broadcast_in_dim.30), channel_id=1, replica_groups=mesh['split'=16,'shard'=8] {'split'}, dimensions={0} | all-to-all | bytes 262144 | tf_op jit(solution)/shard_map/all_to_all | solution.py:18
  61.8 0.1 reduce_max.18
  61.9 7.6 %all_to_all.24 = f32[8,1,2048]{2,1,0:T(1,128)S(1)} all-to-all(f32[8,1,2048]{2,1,0:T(1,128)S(1)} %broadcast_in_dim.31), channel_id=1, replica_groups=mesh['split'=16,'shard'=8] {'shard'}, dimensions={0} | all-to-all | bytes 131072 | tf_op jit(solution)/shard_map/all_to_all | solution.py:18
  69.5 0.7 reduce_max.19
  (12 shorter events, 0.1 us)
Async XLA Ops:
  0.6 21.3 %copy-start = (bf16[1,2,512,400]{2,3,1,0:T(8,128)(2,1)S(1)}, bf16[1,2,512,400]{2,3,1,0:T(8,128)(2,1)}, u32[]{:S(2)}) copy-start(bf16[1,2,512,400]{2,3,1,0:T(8,128)(2,1)} %param.5) | copy-start | bytes 2457604
  0.6 24.9 %copy-start.1 = (bf16[1,50,2048]{2,1,0:T(8,128)(2,1)S(1)}, bf16[1,50,2048]{2,1,0:T(8,128)(2,1)}, u32[]{:S(2)}) copy-start(bf16[1,50,2048]{2,1,0:T(8,128)(2,1)} %param.4) | copy-start | bytes 614404
  0.7 20.0 %collective-permute-start.1 = (bf16[50,2048]{1,0:T(8,128)(2,1)}, bf16[50,2048]{1,0:T(8,128)(2,1)}, u32[]{:S(2)}, u32[]{:S(2)}) collective-permute-start(bf16[50,2048]{1,0:T(8,128)(2,1)} %bitcast.18), channel_id=1, source_target_pairs={{0,2},{1,3},{2,0},{3,1},{4,6},{5,7},{6,4},{7,5},{8,10},{9,11},{10,... | collective-permute-start | bytes 614408 | tf_op jit(solution)/shard_map/ppermute | solution.py:195
  5.2 10.7 %collective-permute-start = (bf16[50,2048]{1,0:T(8,128)(2,1)}, bf16[50,2048]{1,0:T(8,128)(2,1)S(1)}, u32[]{:S(2)}, u32[]{:S(2)}) collective-permute-start(bf16[50,2048]{1,0:T(8,128)(2,1)} %bitcast.19), channel_id=1, source_target_pairs={{0,4},{1,5},{2,6},{3,7},{4,0},{5,1},{6,2},{7,3},{8,12},{9,13},{10,... | collective-permute-start | bytes 614408 | tf_op jit(solution)/shard_map/ppermute | solution.py:195
  6.5 0.7 copy-start.2
  7.8 17.7 %all-to-all-start = ((f32[128,1,96]{2,1,0:T(1,128)}), f32[128,1,96]{2,1,0:T(1,128)S(1)}, u32[]{:S(2)}, u32[]{:S(2)}) async-start(f32[128,1,96]{2,1,0:T(1,128)} %bitcast.1), calls=%async_computation | async-start | bytes 131072 | tf_op jit(solution)/shard_map/all_to_all | solution.py:191
  15.8 16.8 %collective-permute-start.4 = (bf16[50,2048]{1,0:T(8,128)(2,1)}, bf16[50,2048]{1,0:T(8,128)(2,1)S(1)}, u32[]{:S(2)}, u32[]{:S(2)}) collective-permute-start(bf16[50,2048]{1,0:T(8,128)(2,1)} %bitcast.20), channel_id=1, source_target_pairs={{0,3},{1,2},{2,1},{3,0},{4,7},{5,6},{6,5},{7,4},{8,11},{9,10},{10,... | collective-permute-start | bytes 614408 | tf_op jit(solution)/shard_map/ppermute | solution.py:195
  19.2 13.5 %collective-permute-start.3 = (bf16[50,2048]{1,0:T(8,128)(2,1)}, bf16[50,2048]{1,0:T(8,128)(2,1)S(1)}, u32[]{:S(2)}, u32[]{:S(2)}) collective-permute-start(bf16[50,2048]{1,0:T(8,128)(2,1)} %bitcast.21), channel_id=1, source_target_pairs={{0,1},{1,0},{2,3},{3,2},{4,5},{5,4},{6,7},{7,6},{8,9},{9,8},{10,11... | collective-permute-start | bytes 614408 | tf_op jit(solution)/shard_map/ppermute | solution.py:195
  19.2 13.5 %collective-permute-start.6 = (bf16[50,2048]{1,0:T(8,128)(2,1)S(1)}, bf16[50,2048]{1,0:T(8,128)(2,1)S(1)}, u32[]{:S(2)}, u32[]{:S(2)}) collective-permute-start(bf16[50,2048]{1,0:T(8,128)(2,1)S(1)} %collective-permute-done.refs_1_), channel_id=1, source_target_pairs={{0,3},{1,2},{2,1},{3,0},{4,7},{5,6},{6,5},{7,4},{8,11},{9,10},{10,... | collective-permute-start | bytes 614408 | tf_op jit(solution)/shard_map/ppermute | solution.py:195
  19.6 13.1 %collective-permute-start.5 = (bf16[50,2048]{1,0:T(8,128)(2,1)S(1)}, bf16[50,2048]{1,0:T(8,128)(2,1)S(1)}, u32[]{:S(2)}, u32[]{:S(2)}) collective-permute-start(bf16[50,2048]{1,0:T(8,128)(2,1)S(1)} %collective-permute-done.refs_1_), channel_id=1, source_target_pairs={{0,1},{1,0},{2,3},{3,2},{4,5},{5,4},{6,7},{7,6},{8,9},{9,8},{10,11... | collective-permute-start | bytes 614408 | tf_op jit(solution)/shard_map/ppermute | solution.py:195
  20.6 12.0 %collective-permute-start.2 = (bf16[50,2048]{1,0:T(8,128)(2,1)}, bf16[50,2048]{1,0:T(8,128)(2,1)S(1)}, u32[]{:S(2)}, u32[]{:S(2)}) collective-permute-start(bf16[50,2048]{1,0:T(8,128)(2,1)} %collective-permute-done.1.refs_2_), channel_id=1, source_target_pairs={{0,4},{1,5},{2,6},{3,7},{4,0},{5,1},{6,2},{7,3},{8,12},{9,13},{10,... | collective-permute-start | bytes 614408 | tf_op jit(solution)/shard_map/ppermute | solution.py:195

commit v6 on v5

--- a/solution.py
+++ b/solution.py
@@ -62,17 +62,18 @@
 def early_kernel(parts_ref, *refs, blocks):
     block_refs = refs[:blocks]
     out_ref, slab_ref, lines_ref, basis_ref, turned_ref = refs[blocks:]
-    step = pl.program_id(0)
-
-    @pl.when(step == 0)
-    def _():
-        join_strain(parts_ref, lines_ref, turned_ref)
-        for det in range(slab_ref.shape[0]):
-            fill_slab(lines_ref[det : det + 1, :], slab_ref, det)
-        stack_blocks(block_refs, basis_ref)
-
-    for det in range(out_ref.shape[0]):
-        out_ref[det] = filtered(basis_ref, slab_ref, det, step, pl.num_programs(0))
+    ndet, rows, cols = slab_ref.shape
+    taps = basis_ref.shape[1]
+    join_strain(parts_ref, lines_ref, turned_ref)
+    stack_blocks(block_refs, basis_ref)
+    for det in range(ndet):
+        fill_slab(lines_ref[det : det + 1, :], slab_ref, det)
+    for tile in range(out_ref.shape[2] // cols):
+        start = rows - taps - tile * cols
+        for det in range(ndet):
+            frame = slab_ref[det, start : start + taps, :]
+            series = jnp.dot(basis_ref[...], frame, preferred_element_type=jnp.float32)
+            out_ref[det, :, tile * cols : (tile + 1) * cols] = series.astype(jnp.bfloat16)
 
 
 def late_kernel(slab_ref, early_ref, weights_ref, *refs, blocks):
@@ -115,10 +116,9 @@
     nearly = sum(block.shape[0] for block in blocks)
     return pl.pallas_call(
         functools.partial(early_kernel, blocks=len(blocks)),
-        grid=(tout // COLS,),
         in_specs=[pl.BlockSpec(memory_space=VMEM)] * (len(blocks) + 1),
         out_specs=[
-            pl.BlockSpec((ndet, nearly, COLS), lambda i: (0, 0, i)),
+            pl.BlockSpec(memory_space=VMEM),
             pl.BlockSpec(memory_space=VMEM),
         ],
         out_shape=[

time: 70.8 us -> 70.8 us (level)
  no operation moved by 1% of the time
where the time goes in v6:
time: 70.8 us; the launch traced here: 70.1 us
  Pallas kernels  22.7 us (32%)
  blocking collectives  21.7 us (31%)
  starting transfers between devices  19.8 us (28%)
  waiting for transfers between devices  2.85 us (4%)
  matrix products  0.82 us (1%)
  local copies, waits for them, and re-layouts  0.8 us (1%)
  other arithmetic  0.78 us (1%)
  between operations  0.76 us (1%)
    all_to_all x2, blocking collectives, spread(): return lax.all_to_all(copies, axes, 0, 0, tiled=True)  21.7 us
    pallas_call x1, Pallas kernels, bank(): pl.pallas_call(functools.partial(late_kernel, blocks=len(blocks)), grid=(...  15.1 us
    ppermute x7, starting transfers between devices, swap(): return lax.ppermute(block, 'shard', pairs)  11.9 us
    all_to_all x1, starting transfers between devices, per_device(): parts = lax.all_to_all(copies, ('split', 'shard'), 0, 0, tiled=True)  7.91 us
    pallas_call x1, Pallas kernels, early_series(): pl.pallas_call(functools.partial(early_kernel, blocks=len(blocks)), in_sp...  6.88 us
    all_to_all x1, waiting for transfers between devices, per_device(): parts = lax.all_to_all(copies, ('split', 'shard'), 0, 0, tiled=True)  2.83 us
  transfers between devices with their start and end apart: 8, of which 1 were waited for; matrix products, arithmetic and copies ran while one was open for 1% of the time, Pallas kernels for 11%

profile of v6, /device:TPU:1, one launch (start us, length us, event | category | flops | bytes accessed | tf_op | source)
XLA Modules:
  0.0 70.1 jit_solution(5293264470165694600)
XLA Ops:
  0.6 0.0 copy-start
  0.6 0.0 copy-start.1
  0.7 4.5 %collective-permute-start.1 = (bf16[50,2048]{1,0:T(8,128)(2,1)}, bf16[50,2048]{1,0:T(8,128)(2,1)}, u32[]{:S(2)}, u32[]{:S(2)}) collective-permute-start(bf16[50,2048]{1,0:T(8,128)(2,1)} %bitcast.18), channel_id=1, source_target_pairs={{0,2},{1,3},{2,0},{3,1},{4,6},{5,7},{6,4},{7,5},{8,10},{9,11},{10,... | collective-permute-start | bytes 614408 | tf_op jit(solution)/shard_map/ppermute | solution.py:195
  5.2 1.3 %collective-permute-start = (bf16[50,2048]{1,0:T(8,128)(2,1)}, bf16[50,2048]{1,0:T(8,128)(2,1)S(1)}, u32[]{:S(2)}, u32[]{:S(2)}) collective-permute-start(bf16[50,2048]{1,0:T(8,128)(2,1)} %bitcast.19), channel_id=1, source_target_pairs={{0,4},{1,5},{2,6},{3,7},{4,0},{5,1},{6,2},{7,3},{8,12},{9,13},{10,... | collective-permute-start | bytes 614408 | tf_op jit(solution)/shard_map/ppermute | solution.py:195
  6.5 0.7 copy-done.2
  7.1 0.7 %shard_map.50 = f32[128,96]{1,0:T(8,128)} custom-call(bf16[3,32]{1,0:T(4,128)(2,1)S(1)} %copy-done.2), custom_call_target="tpu_custom_call" | custom-call | tf_op jit(solution)/shard_map/pallas_call | solution.py:175
  7.8 7.9 %all-to-all-start = ((f32[128,1,96]{2,1,0:T(1,128)}), f32[128,1,96]{2,1,0:T(1,128)S(1)}, u32[]{:S(2)}, u32[]{:S(2)}) async-start(f32[128,1,96]{2,1,0:T(1,128)} %bitcast.1), calls=%async_computation | async-start | bytes 131072 | tf_op jit(solution)/shard_map/all_to_all | solution.py:191
  15.8 0.0 collective-permute-done.refs_1_
  15.8 3.3 %collective-permute-start.4 = (bf16[50,2048]{1,0:T(8,128)(2,1)}, bf16[50,2048]{1,0:T(8,128)(2,1)S(1)}, u32[]{:S(2)}, u32[]{:S(2)}) collective-permute-start(bf16[50,2048]{1,0:T(8,128)(2,1)} %bitcast.20), channel_id=1, source_target_pairs={{0,3},{1,2},{2,1},{3,0},{4,7},{5,6},{6,5},{7,4},{8,11},{9,10},{10,... | collective-permute-start | bytes 614408 | tf_op jit(solution)/shard_map/ppermute | solution.py:195
  19.2 0.0 collective-permute-start.3
  19.2 0.4 collective-permute-start.6
  19.6 1.1 %collective-permute-start.5 = (bf16[50,2048]{1,0:T(8,128)(2,1)S(1)}, bf16[50,2048]{1,0:T(8,128)(2,1)S(1)}, u32[]{:S(2)}, u32[]{:S(2)}) collective-permute-start(bf16[50,2048]{1,0:T(8,128)(2,1)S(1)} %collective-permute-done.refs_1_), channel_id=1, source_target_pairs={{0,1},{1,0},{2,3},{3,2},{4,5},{5,4},{6,7},{7,6},{8,9},{9,8},{10,11... | collective-permute-start | bytes 614408 | tf_op jit(solution)/shard_map/ppermute | solution.py:195
  20.6 0.0 collective-permute-done.1.refs_2_
  20.6 1.3 %collective-permute-start.2 = (bf16[50,2048]{1,0:T(8,128)(2,1)}, bf16[50,2048]{1,0:T(8,128)(2,1)S(1)}, u32[]{:S(2)}, u32[]{:S(2)}) collective-permute-start(bf16[50,2048]{1,0:T(8,128)(2,1)} %collective-permute-done.1.refs_2_), channel_id=1, source_target_pairs={{0,4},{1,5},{2,6},{3,7},{4,0},{5,1},{6,2},{7,3},{8,12},{9,13},{10,... | collective-permute-start | bytes 614408 | tf_op jit(solution)/shard_map/ppermute | solution.py:195
  21.9 0.8 %convolution_convert_fusion = bf16[512,2,512]{0,2,1:T(8,128)(2,1)S(1)} fusion(bf16[1,2,512,400]{2,3,1,0:T(8,128)(2,1)S(1)} %copy-done, s32[512]{0:T(512)S(1)} %get-tuple-element.13, s32[512]{0:T(512)S(1)} %get-tuple-element.14, s32[]{:T(128)S(6)} %axis_index.12, s32[512]{0:T(512)S(1)} %get-tuple-element.12, s32[512]{0:T(512)S(1)} %get-tuple-element.15, ...), kind=kOutput, calls=%fused_computation.7 | convolution fusion | flops 424255488 | bytes 1877508 | tf_op jit(solution)/shard_map/qml,lp->qmp/dot_general | solution.py:214
  22.7 2.8 %all-to-all-done = f32[128,1,96]{2,1,0:T(1,128)S(1)} async-done(((f32[128,1,96]{2,1,0:T(1,128)}), f32[128,1,96]{2,1,0:T(1,128)S(1)}, u32[]{:S(2)}, u32[]{:S(2)}) %all-to-all-start) | async-done | bytes 49184 | tf_op jit(solution)/shard_map/all_to_all | solution.py:191
  25.6 6.9 %shard_map.51 = (bf16[3,150,2048]{2,1,0:T(8,128)(2,1)S(1)}, bf16[3,3584,512]{2,1,0:T(8,128)(2,1)S(1)}) custom-call(f32[128,96]{1,0:T(8,128)S(1)} %bitcast.17, bf16[50,2048]{1,0:T(8,128)(2,1)S(1)} %bitcast.22, bf16[50,2048]{1,0:T(8,128)(2,1)S(1)} %collective-permute-done.refs_1_, bf16[50,2048]{1,0:T(8,128)(2,1)} %collective-permute-done.1.refs_2_), custom_call_target="tpu_custom_call" | custom-call | tf_op jit(solution)/shard_map/pallas_call | solution.py:117
  32.5 0.0 collective-permute-done.4.refs_2_
  32.5 15.1 %shard_map.52 = (f32[512,2048]{1,0:T(8,128)}, f32[1,2048]{1,0:T(1,128)S(1)}) custom-call(bf16[3,3584,512]{2,1,0:T(8,128)(2,1)S(1)} %get-tuple-element.7.slab_ref, bf16[3,150,2048]{2,1,0:T(8,128)(2,1)S(1)} %get-tuple-element.8.early_ref, bf16[1024,512]{1,0:T(8,128)(2,1)S(1)} %bitcast.16, bf16[50,2048]{1,0:T(8,128)(2,1)S(1)} %collective-permute-done.2.refs_0_, ...), custom_call_target="tpu_custom_call" | custom-call | tf_op jit(solution)/shard_map/pallas_call | solution.py:144
  47.6 0.1 broadcast_in_dim.30
  47.7 14.1 %all_to_all.23 = f32[16,1,2048]{2,1,0:T(1,128)S(1)} all-to-all(f32[16,1,2048]{2,1,0:T(1,128)S(1)} %broadcast_in_dim.30), channel_id=1, replica_groups=mesh['split'=16,'shard'=8] {'split'}, dimensions={0} | all-to-all | bytes 262144 | tf_op jit(solution)/shard_map/all_to_all | solution.py:18
  61.8 0.1 reduce_max.18
  61.9 7.6 %all_to_all.24 = f32[8,1,2048]{2,1,0:T(1,128)S(1)} all-to-all(f32[8,1,2048]{2,1,0:T(1,128)S(1)} %broadcast_in_dim.31), channel_id=1, replica_groups=mesh['split'=16,'shard'=8] {'shard'}, dimensions={0} | all-to-all | bytes 131072 | tf_op jit(solution)/shard_map/all_to_all | solution.py:18
  69.5 0.7 reduce_max.19
  (12 shorter events, 0.1 us)
Async XLA Ops:
  0.6 21.3 %copy-start = (bf16[1,2,512,400]{2,3,1,0:T(8,128)(2,1)S(1)}, bf16[1,2,512,400]{2,3,1,0:T(8,128)(2,1)}, u32[]{:S(2)}) copy-start(bf16[1,2,512,400]{2,3,1,0:T(8,128)(2,1)} %param.5) | copy-start | bytes 2457604
  0.6 24.9 %copy-start.1 = (bf16[1,50,2048]{2,1,0:T(8,128)(2,1)S(1)}, bf16[1,50,2048]{2,1,0:T(8,128)(2,1)}, u32[]{:S(2)}) copy-start(bf16[1,50,2048]{2,1,0:T(8,128)(2,1)} %param.4) | copy-start | bytes 614404
  0.7 20.0 %collective-permute-start.1 = (bf16[50,2048]{1,0:T(8,128)(2,1)}, bf16[50,2048]{1,0:T(8,128)(2,1)}, u32[]{:S(2)}, u32[]{:S(2)}) collective-permute-start(bf16[50,2048]{1,0:T(8,128)(2,1)} %bitcast.18), channel_id=1, source_target_pairs={{0,2},{1,3},{2,0},{3,1},{4,6},{5,7},{6,4},{7,5},{8,10},{9,11},{10,... | collective-permute-start | bytes 614408 | tf_op jit(solution)/shard_map/ppermute | solution.py:195
  5.2 10.7 %collective-permute-start = (bf16[50,2048]{1,0:T(8,128)(2,1)}, bf16[50,2048]{1,0:T(8,128)(2,1)S(1)}, u32[]{:S(2)}, u32[]{:S(2)}) collective-permute-start(bf16[50,2048]{1,0:T(8,128)(2,1)} %bitcast.19), channel_id=1, source_target_pairs={{0,4},{1,5},{2,6},{3,7},{4,0},{5,1},{6,2},{7,3},{8,12},{9,13},{10,... | collective-permute-start | bytes 614408 | tf_op jit(solution)/shard_map/ppermute | solution.py:195
  6.5 0.7 copy-start.2
  7.8 17.7 %all-to-all-start = ((f32[128,1,96]{2,1,0:T(1,128)}), f32[128,1,96]{2,1,0:T(1,128)S(1)}, u32[]{:S(2)}, u32[]{:S(2)}) async-start(f32[128,1,96]{2,1,0:T(1,128)} %bitcast.1), calls=%async_computation | async-start | bytes 131072 | tf_op jit(solution)/shard_map/all_to_all | solution.py:191
  15.8 16.6 %collective-permute-start.4 = (bf16[50,2048]{1,0:T(8,128)(2,1)}, bf16[50,2048]{1,0:T(8,128)(2,1)S(1)}, u32[]{:S(2)}, u32[]{:S(2)}) collective-permute-start(bf16[50,2048]{1,0:T(8,128)(2,1)} %bitcast.20), channel_id=1, source_target_pairs={{0,3},{1,2},{2,1},{3,0},{4,7},{5,6},{6,5},{7,4},{8,11},{9,10},{10,... | collective-permute-start | bytes 614408 | tf_op jit(solution)/shard_map/ppermute | solution.py:195
  19.2 13.3 %collective-permute-start.3 = (bf16[50,2048]{1,0:T(8,128)(2,1)}, bf16[50,2048]{1,0:T(8,128)(2,1)S(1)}, u32[]{:S(2)}, u32[]{:S(2)}) collective-permute-start(bf16[50,2048]{1,0:T(8,128)(2,1)} %bitcast.21), channel_id=1, source_target_pairs={{0,1},{1,0},{2,3},{3,2},{4,5},{5,4},{6,7},{7,6},{8,9},{9,8},{10,11... | collective-permute-start | bytes 614408 | tf_op jit(solution)/shard_map/ppermute | solution.py:195
  19.2 13.3 %collective-permute-start.6 = (bf16[50,2048]{1,0:T(8,128)(2,1)S(1)}, bf16[50,2048]{1,0:T(8,128)(2,1)S(1)}, u32[]{:S(2)}, u32[]{:S(2)}) collective-permute-start(bf16[50,2048]{1,0:T(8,128)(2,1)S(1)} %collective-permute-done.refs_1_), channel_id=1, source_target_pairs={{0,3},{1,2},{2,1},{3,0},{4,7},{5,6},{6,5},{7,4},{8,11},{9,10},{10,... | collective-permute-start | bytes 614408 | tf_op jit(solution)/shard_map/ppermute | solution.py:195
  19.6 12.9 %collective-permute-start.5 = (bf16[50,2048]{1,0:T(8,128)(2,1)S(1)}, bf16[50,2048]{1,0:T(8,128)(2,1)S(1)}, u32[]{:S(2)}, u32[]{:S(2)}) collective-permute-start(bf16[50,2048]{1,0:T(8,128)(2,1)S(1)} %collective-permute-done.refs_1_), channel_id=1, source_target_pairs={{0,1},{1,0},{2,3},{3,2},{4,5},{5,4},{6,7},{7,6},{8,9},{9,8},{10,11... | collective-permute-start | bytes 614408 | tf_op jit(solution)/shard_map/ppermute | solution.py:195
  20.6 11.8 %collective-permute-start.2 = (bf16[50,2048]{1,0:T(8,128)(2,1)}, bf16[50,2048]{1,0:T(8,128)(2,1)S(1)}, u32[]{:S(2)}, u32[]{:S(2)}) collective-permute-start(bf16[50,2048]{1,0:T(8,128)(2,1)} %collective-permute-done.1.refs_2_), channel_id=1, source_target_pairs={{0,4},{1,5},{2,6},{3,7},{4,0},{5,1},{6,2},{7,3},{8,12},{9,13},{10,... | collective-permute-start | bytes 614408 | tf_op jit(solution)/shard_map/ppermute | solution.py:195
